TPU v7x, 32 devices: a whole 2x2x4 slice. The times are simulated.
32 devices in a mesh: rep: 8 (over y, x, core), fsdp: 4 (over z).
Axes of the slice: x: 2, y: 2, z: 4, core: 2. Of those that a mesh axis runs over, the one named last changes fastest.
Arguments:
- tokens: bfloat16 [32768, 768], P(('rep', 'fsdp')), may hold values from -11 to 11
- segments: int32 [32768], P(('rep', 'fsdp')), may hold values from -1 to 1, as said below
- random_blocks: int32 [32, 16, 3], P(('rep', 'fsdp')), may hold values from 0 to 15, as said below
- out_grad: bfloat16 [32768, 768], P(('rep', 'fsdp')), may hold values from -6 to 6
- w_query: bfloat16 [768, 768], P('fsdp'), may hold values from -0.21875 to 0.21875
- w_key: bfloat16 [768, 768], P('fsdp'), may hold values from -0.21875 to 0.21875
- w_value: bfloat16 [768, 768], P('fsdp'), may hold values from -0.21875 to 0.21875
- w_out: bfloat16 [768, 768], P('fsdp'), may hold values from -0.875 to 0.875
- w_up: bfloat16 [768, 3072], P('fsdp'), may hold values from -0.21875 to 0.21875
- w_down: bfloat16 [3072, 768], P('fsdp'), may hold values from -0.109375 to 0.109375
- vectors: bfloat16 [8, 768], P(None, 'fsdp'), may hold values from -1.5 to 1.5
- up_bias: bfloat16 [3072], P('fsdp'), may hold values from -1 to 1
Outputs:
- layer_out: bfloat16 [32768, 768], P(('rep', 'fsdp'))
- tokens_grad: bfloat16 [32768, 768], P(('rep', 'fsdp'))
- w_query_grad: float32 [768, 768], P('fsdp')
- w_key_grad: float32 [768, 768], P('fsdp')
- w_value_grad: float32 [768, 768], P('fsdp')
- w_out_grad: float32 [768, 768], P('fsdp')
- w_up_grad: float32 [768, 3072], P('fsdp')
- w_down_grad: float32 [3072, 768], P('fsdp')
- vectors_grad: float32 [8, 768], P(None, 'fsdp')
- up_bias_grad: float32 [3072], P('fsdp')
- rms_values: float32 [3], replicated
Inputs may be any that keep to these rules, and one draw needn't show every extreme that they name: `segments`: in each sequence the tokens that are not padding come first with segment numbers that never fall and take every value 0 to 1; the rest are -1, and every sequence has some. `random_blocks`: for query block b >= 2 of a sequence, three distinct block numbers, none of them 0, 1, b - 1, b or b + 1; the rows of blocks 0 and 1 are not read.
All inputs are finite; a program needn't handle non-finite values.
Results may differ from a plain program's by a relative error of at most 0.017.
Values may be sent and summed in bfloat16 or wider, within the bound.
A program may use at most 320 MiB of HBM per device.

v0:
```python
import jax
import jax.numpy as jnp
from jax import lax
from jax.sharding import PartitionSpec as P

D = 768
H = 12
DH = 64
BLK = 64
SEQ_LEN = 1024
NB = 16


masked_score = -1e30
layer_eps = 1e-05


def normalize(values, gain, shift):
    centered = values - jnp.mean(values, axis=-1, keepdims=True)
    variance = jnp.mean(centered * centered, axis=-1, keepdims=True)
    return centered * lax.rsqrt(variance + layer_eps) * gain + shift


def gelu_exact(values):
    return jax.nn.gelu(values, approximate=False)


def dot_tn(left, right):
    return lax.dot_general(
        left, right, (((0,), (0,)), ((), ())), preferred_element_type=jnp.float32
    )


def dot_nt(left, right):
    return lax.dot_general(
        left, right, (((1,), (1,)), ((), ())), preferred_element_type=jnp.float32
    )


def col_sums(values):
    return jnp.sum(values.astype(jnp.float32), axis=0)


def slot_tables(random_row):
    later = jnp.arange(2, NB, dtype=jnp.int32)
    zeros_col = jnp.zeros_like(later)
    slot_table = jnp.stack(
        [
            zeros_col,
            zeros_col + 1,
            later - 1,
            later,
            jnp.minimum(later + 1, NB - 1),
            random_row[2:, 0],
            random_row[2:, 1],
            random_row[2:, 2],
        ],
        axis=1,
    )
    always = later >= 0
    slot_ok = jnp.stack(
        [always, always, later >= 3, always, later <= NB - 2, always, always, always], axis=1
    )
    return (slot_table, slot_ok)


def visibility(seg_row, slot_table, slot_ok):
    seg_blocks = seg_row.reshape(NB, BLK)
    seg_picked = jnp.take(seg_blocks, slot_table, axis=0)
    local_seen = slot_ok[:, None, :, None] & (
        seg_blocks[2:][:, :, None, None] == seg_picked[:, None, :, :]
    )
    local_seen = local_seen.reshape(NB - 2, 1, BLK, 8 * BLK)
    global_seen = (seg_row[: 2 * BLK][:, None] == seg_row[None, :])[None]
    return (local_seen, global_seen)


def log_norm(scores):
    row_max = jnp.max(scores, axis=-1, keepdims=True)
    return row_max + jnp.log(jnp.sum(jnp.exp(scores - row_max), axis=-1, keepdims=True))


def prepare(q_seq, k_seq, v_seq, seg_row, random_row):
    slot_table, slot_ok = slot_tables(random_row)
    local_seen, global_seen = visibility(seg_row, slot_table, slot_ok)
    q_heads = q_seq.reshape(NB, BLK, H, DH)
    k_picked = jnp.take(k_seq.reshape(NB, BLK, H, DH), slot_table, axis=0)
    v_picked = jnp.take(v_seq.reshape(NB, BLK, H, DH), slot_table, axis=0)
    scores = (
        jnp.einsum("nqhd,nsjhd->nhqsj", q_heads[2:], k_picked, preferred_element_type=jnp.float32)
        * 0.125
    )
    scores = jnp.where(local_seen, scores.reshape(NB - 2, H, BLK, 8 * BLK), masked_score)
    q_glob = q_seq[: 2 * BLK].reshape(2 * BLK, H, DH)
    k_all = k_seq.reshape(SEQ_LEN, H, DH)
    v_all = v_seq.reshape(SEQ_LEN, H, DH)
    g_scores = jnp.einsum("qhd,khd->hqk", q_glob, k_all, preferred_element_type=jnp.float32) * 0.125
    g_scores = jnp.where(global_seen, g_scores, masked_score)
    return (slot_table, q_heads, k_picked, v_picked, scores, q_glob, k_all, v_all, g_scores)


def attend_forward(group):
    q_seq, k_seq, v_seq, seg_row, random_row = group
    slot_table, q_heads, k_picked, v_picked, scores, q_glob, k_all, v_all, g_scores = prepare(
        q_seq, k_seq, v_seq, seg_row, random_row
    )
    local_log = log_norm(scores)
    probs_low = jnp.exp(scores - local_log).astype(jnp.bfloat16).reshape(NB - 2, H, BLK, 8, BLK)
    local_out = jnp.einsum(
        "nhqsj,nsjhd->nqhd", probs_low, v_picked, preferred_element_type=jnp.float32
    )
    global_log = log_norm(g_scores)
    g_probs_low = jnp.exp(g_scores - global_log).astype(jnp.bfloat16)
    global_out = jnp.einsum("hqk,khd->qhd", g_probs_low, v_all, preferred_element_type=jnp.float32)
    attended = jnp.concatenate(
        [global_out.reshape(2 * BLK, D), local_out.reshape((NB - 2) * BLK, D)], axis=0
    )
    return (attended, local_log, global_log)


def attend_backward(group):
    q_seq, k_seq, v_seq, seg_row, random_row, local_log, global_log, d_seq = group
    slot_table, q_heads, k_picked, v_picked, scores, q_glob, k_all, v_all, g_scores = prepare(
        q_seq, k_seq, v_seq, seg_row, random_row
    )
    probs = jnp.exp(scores - local_log)
    d_heads = d_seq.reshape(NB, BLK, H, DH)
    d_probs = jnp.einsum(
        "nqhd,nsjhd->nhqsj", d_heads[2:], v_picked, preferred_element_type=jnp.float32
    )
    d_probs = d_probs.reshape(NB - 2, H, BLK, 8 * BLK)
    inner_sum = jnp.sum(probs * d_probs, axis=-1, keepdims=True)
    d_scores = (probs * (d_probs - inner_sum)).astype(jnp.bfloat16).reshape(NB - 2, H, BLK, 8, BLK)
    probs_low = probs.astype(jnp.bfloat16).reshape(NB - 2, H, BLK, 8, BLK)
    dq_local = 0.125 * jnp.einsum(
        "nhqsj,nsjhd->nqhd", d_scores, k_picked, preferred_element_type=jnp.float32
    )
    dk_picked = 0.125 * jnp.einsum(
        "nhqsj,nqhd->nsjhd", d_scores, q_heads[2:], preferred_element_type=jnp.float32
    )
    dv_picked = jnp.einsum(
        "nhqsj,nqhd->nsjhd", probs_low, d_heads[2:], preferred_element_type=jnp.float32
    )
    selector = (slot_table[:, :, None] == jnp.arange(NB, dtype=jnp.int32)[None, None, :]).astype(
        jnp.float32
    )
    dk_blocks = jnp.einsum("nsb,nsjhd->bjhd", selector, dk_picked, precision=lax.Precision.HIGHEST)
    dv_blocks = jnp.einsum("nsb,nsjhd->bjhd", selector, dv_picked, precision=lax.Precision.HIGHEST)
    g_probs = jnp.exp(g_scores - global_log)
    d_glob = d_seq[: 2 * BLK].reshape(2 * BLK, H, DH)
    g_dprobs = jnp.einsum("qhd,khd->hqk", d_glob, v_all, preferred_element_type=jnp.float32)
    g_inner = jnp.sum(g_probs * g_dprobs, axis=-1, keepdims=True)
    g_dscores = (g_probs * (g_dprobs - g_inner)).astype(jnp.bfloat16)
    dq_glob = 0.125 * jnp.einsum(
        "hqk,khd->qhd", g_dscores, k_all, preferred_element_type=jnp.float32
    )
    dk_glob = 0.125 * jnp.einsum(
        "hqk,qhd->khd", g_dscores, q_glob, preferred_element_type=jnp.float32
    )
    dv_glob = jnp.einsum(
        "hqk,qhd->khd", g_probs.astype(jnp.bfloat16), d_glob, preferred_element_type=jnp.float32
    )
    d_query = jnp.concatenate(
        [dq_glob.reshape(2 * BLK, D), dq_local.reshape((NB - 2) * BLK, D)], axis=0
    )
    d_key = dk_blocks.reshape(SEQ_LEN, D) + dk_glob.reshape(SEQ_LEN, D)
    d_value = dv_blocks.reshape(SEQ_LEN, D) + dv_glob.reshape(SEQ_LEN, D)
    return (d_query, d_key, d_value)


def per_device(
    tokens,
    segments,
    random_blocks,
    out_grad,
    w_query,
    w_key,
    w_value,
    w_out,
    w_up,
    w_down,
    vectors,
    up_bias,
):
    gathered = (
        lax.all_gather(w_query, "fsdp", axis=0, tiled=True),
        lax.all_gather(w_key, "fsdp", axis=0, tiled=True),
        lax.all_gather(w_value, "fsdp", axis=0, tiled=True),
        lax.all_gather(w_out, "fsdp", axis=0, tiled=True),
        lax.all_gather(w_up, "fsdp", axis=0, tiled=True),
        lax.all_gather(w_down, "fsdp", axis=0, tiled=True),
        lax.all_gather(vectors, "fsdp", axis=1, tiled=True),
        lax.all_gather(up_bias, "fsdp", axis=0, tiled=True),
    )
    full_query, full_key, full_value, full_out, full_up, full_down, full_vectors, full_upbias = (
        gathered
    )
    vec_float = full_vectors.astype(jnp.float32)
    inputs = tokens.astype(jnp.float32)
    q_low = (jnp.dot(tokens, full_query, preferred_element_type=jnp.float32) + vec_float[0]).astype(
        jnp.bfloat16
    )
    k_low = jnp.dot(tokens, full_key, preferred_element_type=jnp.float32).astype(jnp.bfloat16)
    v_low = (jnp.dot(tokens, full_value, preferred_element_type=jnp.float32) + vec_float[1]).astype(
        jnp.bfloat16
    )
    seq_q = q_low.reshape(-1, SEQ_LEN, D)
    seq_k = k_low.reshape(-1, SEQ_LEN, D)
    seq_v = v_low.reshape(-1, SEQ_LEN, D)
    seq_seg = segments.reshape(-1, SEQ_LEN)
    attended, local_logs, global_logs = lax.map(
        attend_forward, (seq_q, seq_k, seq_v, seq_seg, random_blocks)
    )
    mixed_low = attended.reshape(-1, D).astype(jnp.bfloat16)
    attn_out = jnp.dot(mixed_low, full_out, preferred_element_type=jnp.float32) + vec_float[2]
    first_sum = inputs + attn_out
    normed_one, pull_one = jax.vjp(normalize, first_sum, vec_float[3], vec_float[4])
    normed_low = normed_one.astype(jnp.bfloat16)
    up_proj = jnp.dot(normed_low, full_up, preferred_element_type=jnp.float32) + full_upbias.astype(
        jnp.float32
    )
    activated, pull_gelu = jax.vjp(gelu_exact, up_proj)
    activated_low = activated.astype(jnp.bfloat16)
    mlp_out = jnp.dot(activated_low, full_down, preferred_element_type=jnp.float32) + vec_float[5]
    second_sum = normed_one + mlp_out
    layer_out, pull_two = jax.vjp(normalize, second_sum, vec_float[6], vec_float[7])
    valid = (segments >= 0).astype(jnp.float32)[:, None]
    squares = jnp.stack(
        [
            jnp.sum(valid * first_sum * first_sum),
            jnp.sum(valid * attn_out * attn_out),
            jnp.sum(valid * mlp_out * mlp_out),
        ]
    )
    squares, counted = lax.psum((squares, jnp.sum(valid)), ("rep", "fsdp"))
    rms_values = jnp.sqrt(squares / (counted * D))
    regathered = (
        lax.all_gather(w_query, "fsdp", axis=0, tiled=True),
        lax.all_gather(w_key, "fsdp", axis=0, tiled=True),
        lax.all_gather(w_value, "fsdp", axis=0, tiled=True),
        lax.all_gather(w_out, "fsdp", axis=0, tiled=True),
        lax.all_gather(w_up, "fsdp", axis=0, tiled=True),
        lax.all_gather(w_down, "fsdp", axis=0, tiled=True),
    )
    back_query, back_key, back_value, back_out, back_up, back_down = regathered
    d_second, d_gain_two, d_shift_two = pull_two(out_grad.astype(jnp.float32))
    d_mlp = d_second.astype(jnp.bfloat16)
    d_up = pull_gelu(dot_nt(d_mlp, back_down))[0].astype(jnp.bfloat16)
    d_normed = d_second + dot_nt(d_up, back_up)
    d_first, d_gain_one, d_shift_one = pull_one(d_normed)
    d_attn = d_first.astype(jnp.bfloat16)
    d_mixed = dot_nt(d_attn, back_out).astype(jnp.bfloat16)
    d_query, d_key, d_value = lax.map(
        attend_backward,
        (
            seq_q,
            seq_k,
            seq_v,
            seq_seg,
            random_blocks,
            local_logs,
            global_logs,
            d_mixed.reshape(-1, SEQ_LEN, D),
        ),
    )
    dq_low = d_query.reshape(-1, D).astype(jnp.bfloat16)
    dk_low = d_key.reshape(-1, D).astype(jnp.bfloat16)
    dv_low = d_value.reshape(-1, D).astype(jnp.bfloat16)
    tokens_grad = (
        d_first + dot_nt(dq_low, back_query) + dot_nt(dk_low, back_key) + dot_nt(dv_low, back_value)
    )
    grad_query = dot_tn(tokens, dq_low)
    grad_key = dot_tn(tokens, dk_low)
    grad_value = dot_tn(tokens, dv_low)
    grad_out = dot_tn(mixed_low, d_attn)
    grad_up = dot_tn(normed_low, d_up)
    grad_down = dot_tn(activated_low, d_mlp)
    grad_vectors = jnp.stack(
        [
            col_sums(dq_low),
            col_sums(dv_low),
            col_sums(d_attn),
            d_gain_one,
            d_shift_one,
            col_sums(d_mlp),
            d_gain_two,
            d_shift_two,
        ]
    )
    grad_upbias = col_sums(d_up)
    shard_sums = (
        lax.psum_scatter(
            grad_query.astype(jnp.bfloat16), "fsdp", scatter_dimension=0, tiled=True
        ).astype(jnp.float32),
        lax.psum_scatter(
            grad_key.astype(jnp.bfloat16), "fsdp", scatter_dimension=0, tiled=True
        ).astype(jnp.float32),
        lax.psum_scatter(
            grad_value.astype(jnp.bfloat16), "fsdp", scatter_dimension=0, tiled=True
        ).astype(jnp.float32),
        lax.psum_scatter(
            grad_out.astype(jnp.bfloat16), "fsdp", scatter_dimension=0, tiled=True
        ).astype(jnp.float32),
        lax.psum_scatter(
            grad_up.astype(jnp.bfloat16), "fsdp", scatter_dimension=0, tiled=True
        ).astype(jnp.float32),
        lax.psum_scatter(
            grad_down.astype(jnp.bfloat16), "fsdp", scatter_dimension=0, tiled=True
        ).astype(jnp.float32),
        lax.psum_scatter(
            grad_vectors.astype(jnp.bfloat16), "fsdp", scatter_dimension=1, tiled=True
        ).astype(jnp.float32),
        lax.psum_scatter(
            grad_upbias.astype(jnp.bfloat16), "fsdp", scatter_dimension=0, tiled=True
        ).astype(jnp.float32),
    )
    results = lax.psum(
        (
            shard_sums[0],
            shard_sums[1],
            shard_sums[2],
            shard_sums[3],
            shard_sums[4],
            shard_sums[5],
            shard_sums[6],
            shard_sums[7],
        ),
        "rep",
    )
    return (
        layer_out.astype(jnp.bfloat16),
        tokens_grad.astype(jnp.bfloat16),
        results[0],
        results[1],
        results[2],
        results[3],
        results[4],
        results[5],
        results[6],
        results[7],
        rms_values,
    )


def solution(mesh):
    in_specs = (
        P(("rep", "fsdp"), None),
        P(("rep", "fsdp")),
        P(("rep", "fsdp"), None, None),
        P(("rep", "fsdp"), None),
        P("fsdp", None),
        P("fsdp", None),
        P("fsdp", None),
        P("fsdp", None),
        P("fsdp", None),
        P("fsdp", None),
        P(None, "fsdp"),
        P("fsdp"),
    )
    out_specs = (
        P(("rep", "fsdp"), None),
        P(("rep", "fsdp"), None),
        P("fsdp", None),
        P("fsdp", None),
        P("fsdp", None),
        P("fsdp", None),
        P("fsdp", None),
        P("fsdp", None),
        P(None, "fsdp"),
        P("fsdp"),
        P(),
    )
    return jax.shard_map(
        per_device, mesh=mesh, in_specs=in_specs, out_specs=out_specs, check_vma=False
    )
```

profile of v0, /device:TPU:0, one launch (start us, length us, event | category | flops | bytes accessed | tf_op | source)
XLA Modules:
  0.0 1196.4 jit_solution(7031458401899841001)
XLA Ops:
  15.7 15.2 %all-gather.1 = bf16[4,1,768]{2,1,0:T(2,128)(2,1)S(1)} all-gather(bf16[1,1,768]{2,1,0:T(2,128)(2,1)S(1)} %reshape.421), channel_id=1, replica_groups=mesh['rep'=8,'fsdp'=4] {'fsdp'}, dimensions={0}, use_global_device_ids=true | all-gather | bytes 7680 | tf_op jit(solution)/shard_map/all_gather | solution.py:193
  31.5 13.5 %all-gather = bf16[4,192,8]{1,2,0:T(8,128)(2,1)S(1)} all-gather(bf16[1,192,8]{1,2,0:T(8,128)(2,1)S(1)} %bitcast.201), channel_id=1, replica_groups=mesh['rep'=8,'fsdp'=4] {'fsdp'}, dimensions={0}, use_global_device_ids=true | all-gather | bytes 15360 | tf_op jit(solution)/shard_map/all_gather | solution.py:192
  58.1 16.0 %all-gather.13.cloned.1.call-done = bf16[768,768]{1,0:T(8,128)(2,1)} async-done(((bf16[192,768]{1,0:T(8,128)(2,1)}), bf16[768,768]{1,0:T(8,128)(2,1)}) %all-gather.13.cloned.1.call-update) | async-done | bytes 1179664 | tf_op jit(solution)/shard_map/all_gather | solution.py:187
  81.2 3.9 copy.94
  85.2 20.0 %all-gather.9.cloned.1.call-done = bf16[768,768]{1,0:T(8,128)(2,1)} async-done(((bf16[192,768]{1,0:T(8,128)(2,1)}), bf16[768,768]{1,0:T(8,128)(2,1)}) %all-gather.9.cloned.1.call-update) | async-done | bytes 1179664 | tf_op jit(solution)/shard_map/all_gather | solution.py:188
  105.2 4.3 add_convert_fusion.5
  109.5 5.3 reshape.369
  114.8 5.1 copy.88
  125.8 11.9 gather_fusion
  137.7 21.7 %gather_fusion.2 = bf16[112,64,12,64]{3,1,2,0:T(8,128)(2,1)} fusion(bf16[16,64,12,64]{3,1,2,0:T(8,128)(2,1)S(1)} %copy.94, s32[1024]{0:T(1024)S(1)} %pad_clamp_fusion), kind=kCustom, calls=%fused_computation.2.clone | custom fusion | bytes 22020544 | tf_op jit(solution)/shard_map/while/body/eval_jaxpr/jit(_take)/gather | solution.py:87
  159.3 30.4 %broadcast_select_fusion.1 = (bf16[14,8,64,12,64]{4,2,3,1,0:T(8,128)(2,1)}, bf16[14,8,64,12,64]{4,2,3,1,0:T(8,128)(2,1)}) fusion(bf16[14,8,64,12,64]{4,2,3,1,0:T(8,128)(2,1)} %bitcast.178, pred[14,8]{1,0:T(8,128)(4,1)S(1)} %copy.86, bf16[14,8,64,12,64]{4,2,3,1,0:T(8,128)(2,1)} %bitcast.179), kind=kLoop, calls=%fused_computation.12 | loop fusion | flops 11010048 | bytes 44040304 | tf_op jit(solution)/shard_map/while/body/eval_jaxpr/jit(_take)/select_n | solution.py:88
  189.7 22.4 %copy.125 = bf16[14,8,64,12,64]{4,2,1,3,0:T(8,128)(2,1)} copy(bf16[14,8,64,12,64]{4,2,3,1,0:T(8,128)(2,1)} %get-tuple-element.154) | data formatting | bytes 22020096 | tf_op jit(solution)/shard_map/while/body/eval_jaxpr/jit(_take)/select_n | solution.py:88
  212.2 8.2 copy.96
  220.3 23.6 %fusion = (f32[14,12,64]{2,1,0:T(8,128)S(1)}, f32[14,12,64,512]{2,3,1,0}) fusion(pred[14,64,8,64]{1,3,2,0:T(8,128)(4,1)S(1)} %copy-done.2, bf16[14,12,64,512]{2,3,1,0:T(8,128)(2,1)} %bitcast.181, bf16[14,64,12,64]{1,0,3,2:T(8,128)(2,1)S(1)} %copy-done.4), kind=kOutput, calls=%fused_computation.9 | convolution fusion | flops 721147392 | bytes 34908160
  244.0 20.6 %exponential_reduce_fusion = f32[14,12,64]{2,1,0:T(8,128)S(1)} fusion(f32[14,12,64,512]{2,3,1,0} %get-tuple-element.157, f32[14,12,64]{2,1,0:T(8,128)S(1)} %get-tuple-element.156, pred[14,64,8,64]{1,3,2,0:T(8,128)(4,1)S(1)} %copy-done.2), kind=kLoop, calls=%fused_computation.7 | loop fusion | flops 22009344 | bytes 22564864 | tf_op jit(solution)/shard_map/while/body/eval_jaxpr/reduce_sum | solution.py:80
  265.2 25.4 %fusion.21 = bf16[14,64,12,64]{1,3,2,0:T(8,128)(2,1)} fusion(f32[14,12,64,512]{2,3,1,0} %get-tuple-element.157, f32[14,12,64]{2,1,0:T(8,128)S(1)} %log_add_fusion, pred[14,64,8,64]{1,3,2,0:T(8,128)(4,1)S(1)} %copy-done.2, bf16[14,8,64,12,64]{4,2,3,1,0:T(8,128)(2,1)} %get-tuple-element.154), kind=kOutput, calls=%fused_computation.78 | convolution fusion | flops 727351296 | bytes 34908160 | tf_op jit(solution)/shard_map/while/body/eval_jaxpr/nhqsj,nsjhd->nqhd/dot_general | solution.py:109
  290.6 3.9 copy.99
  297.6 4.9 convolution_convert_fusion.8
  302.5 5.5 fusion.72
  308.8 38.1 %multiply_convert_fusion.1 = (bf16[1024,3072]{1,0:T(8,128)(2,1)}, f32[1024,3072]{1,0:T(8,128)}, f32[1024,3072]{1,0:T(8,128)}) fusion(f32[3072]{0:T(1024)S(1)} %bitcast.198, bf16[768,3072]{1,0:T(8,128)(2,1)} %all-gather.17.cloned.1.call-done, f32[1024,768]{0,1:T(8,128)S(1)} %get-tuple-element.148, f32[768]{0:T(1024)S(1)} %copy-done.67, ...), kind=kOutput, calls=%fused_computation.17 | convolution fusion | flops 5043388416 | bytes 39348224 | tf_op jit(solution)/shard_map/dot_general | solution.py:219
  346.9 13.3 %fusion.16 = (f32[]{:T(128)}, f32[]{:T(128)}, f32[1024]{0:T(1024)S(1)}, f32[1024,768]{0,1:T(8,128)S(1)}) fusion(f32[1024,768]{0,1:T(8,128)} %get-tuple-element.160, f32[1024]{0:T(1024)S(1)} %copy-done.72, f32[768]{0:T(1024)S(1)} %copy-done.70, f32[768]{0:T(1024)S(1)} %copy-done.69, f32[768]{0:T(1024)S(1)} %copy-done.67, f32[768]{0:T(1024)S(1)} %copy-done.54, ...), kind=kOutput, calls=%fused_computation.57 | convolution fusion | flops 4842847232 | bytes 20475912 | tf_op jit(solution)/shard_map/dot_general | solution.py:224
  365.2 18.1 %fusion.74 = (bf16[3072]{0:T(1024)(128)(2,1)}, bf16[1024,3072]{1,0:T(8,128)(2,1)}) fusion(f32[1024,3072]{1,0:T(8,128)} %get-tuple-element.146, bf16[1024,768]{0,1:T(8,128)(2,1)S(1)} %get-tuple-element.138, bf16[3072,768]{1,0:T(8,128)(2,1)} %all-gather.19.cloned.1.call-done, f32[1024,3072]{1,0:T(8,128)} %get-tuple-element.161, f32[3072]{0:T(1024)S(1)} %bitcast.199), kind=kOutput, calls=%fused_computation.171 | convolution fusion | flops 4882166784 | bytes 37767168 | tf_op jit(solution)/shard_map/dot_general | solution.py:35
  383.4 11.9 multiply_reduce_fusion.2
  403.6 4.5 multiply_reduce_fusion.1
  411.0 5.0 slice.111
  416.1 5.6 multiply_convert_fusion.2
  429.0 7.7 copy.119
  436.7 38.7 %multiply_reduce_fusion = (f32[14,12,64]{2,1,0:T(8,128)S(1)}, f32[14,12,64,512]{2,3,1,0}) fusion(f32[14,12,64,512]{2,3,1,0} %get-tuple-element.157, f32[14,12,64]{2,1,0:T(8,128)S(1)} %copy-done.28, pred[14,64,8,64]{1,3,2,0:T(8,128)(4,1)S(1)} %copy-done.3, bf16[14,12,64,512]{2,3,1,0:T(8,128)(2,1)} %bitcast.180, bf16[14,64,12,64]{1,0,3,2:T(8,128)(2,1)} %slice.111), kind=kOutput, calls=%fused_computation.5 | convolution fusion | flops 732157440 | bytes 56971264
  475.4 35.4 %multiply_convert_fusion = bf16[14,12,64,8,64]{2,4,3,1,0:T(8,128)(2,1)} fusion(f32[14,12,64,512]{2,3,1,0} %get-tuple-element.157, f32[14,12,64]{2,1,0:T(8,128)S(1)} %get-tuple-element.163, f32[14,12,64]{2,1,0:T(8,128)S(1)} %copy-done.28, pred[14,64,8,64]{1,3,2,0:T(8,128)(4,1)S(1)} %copy-done.3, f32[14,12,64,512]{2,3,1,0} %get-tuple-element.164), kind=kLoop, calls=%fused_computation.4 | loop fusion | flops 33030144 | bytes 55595008 | tf_op jit(solution)/shard_map/while/body/eval_jaxpr/convert_element_type | solution.py:133
  510.8 18.1 %fusion.73 = (bf16[12,64]{1,0:T(8,128)(2,1)S(1)}, bf16[14,64,12,64]{3,1,2,0:T(8,128)(2,1)}) fusion(bf16[14,12,64,8,64]{2,4,3,1,0:T(8,128)(2,1)} %multiply_convert_fusion, bf16[14,8,64,12,64]{4,2,3,1,0:T(8,128)(2,1)} %get-tuple-element.155), kind=kOutput, calls=%fused_computation.170 | convolution fusion | flops 706706688 | bytes 23397888 | tf_op jit(solution)/shard_map/while/body/eval_jaxpr/nhqsj,nsjhd->nqhd/dot_general | solution.py:135
  528.9 37.6 %convolution_bitcast_fusion = f32[14,8,64,12,64]{2,4,1,3,0:T(8,128)} fusion(bf16[14,64,12,64,1]{1,0,3,2,4:T(8,128)(2,1)} %bitcast.184, f32[14,12,64,512]{2,3,1,0} %get-tuple-element.157, f32[14,12,64]{2,1,0:T(8,128)S(1)} %copy-done.28, pred[14,64,8,64]{1,3,2,0:T(8,128)(4,1)S(1)} %copy-done.3), kind=kOutput, calls=%fused_computation.14 | convolution fusion | flops 726663168 | bytes 45918208 | tf_op jit(solution)/shard_map/while/body/eval_jaxpr/nhqsj,nqhd->nsjhd/dot_general | solution.py:141
  566.6 4.1 copy.106
  573.7 49.0 %copy.116 = f32[14,8,64,12,64]{4,0,1,3,2:T(8,128)} copy(f32[14,8,64,12,64]{2,4,1,3,0:T(8,128)} %convolution_bitcast_fusion) | data formatting | bytes 44040192 | tf_op jit(solution)/shard_map/while/body/eval_jaxpr/nhqsj,nqhd->nsjhd/transpose | solution.py:141
  622.7 30.6 %fusion.18 = (bf16[12,64]{1,0:T(8,128)(2,1)S(1)}, f32[16,64,12,64]{3,0,2,1:T(8,128)}) fusion(f32[16,64,12,64]{3,0,2,1:T(8,128)} %copy.119, f32[14,8,64,12,64]{4,0,1,3,2:T(8,128)} %copy.116, s32[14,8]{0,1:T(8,128)S(1)} %copy-done.46), kind=kOutput, calls=%fused_computation.59 | convolution fusion | flops 1059324928 | bytes 28313536 | tf_op jit(solution)/shard_map/while/body/eval_jaxpr/nsb,nsjhd->bjhd/dot_general | solution.py:148
  654.4 7.8 copy.117
  662.2 6.5 reshape.378
  681.1 22.0 %multiply_bitcast_fusion = f32[14,8,64,12,64]{4,2,1,3,0:T(8,128)} fusion(bf16[14,12,64,8,64]{2,4,3,1,0:T(8,128)(2,1)} %multiply_convert_fusion, bf16[14,64,12,64,1]{1,0,3,2,4:T(8,128)(2,1)S(1)} %bitcast.182), kind=kOutput, calls=%fused_computation.3 | convolution fusion | flops 710148096 | bytes 34406400 | tf_op jit(solution)/shard_map/while/body/eval_jaxpr/nhqsj,nqhd->nsjhd/dot_general | solution.py:138
  703.1 49.0 %copy.136 = f32[14,8,64,12,64]{2,0,1,4,3:T(8,128)} copy(f32[14,8,64,12,64]{4,2,1,3,0:T(8,128)} %multiply_bitcast_fusion) | data formatting | bytes 44040192 | tf_op jit(solution)/shard_map/while/body/eval_jaxpr/mul | solution.py:138
  752.2 30.3 %convolution_bitcast_fusion.2 = f32[16,64,12,64]{1,0,3,2:T(8,128)} fusion(f32[14,8,64,12,64]{2,0,1,4,3:T(8,128)} %copy.136, s32[14,8]{0,1:T(8,128)S(1)} %copy-done.46), kind=kOutput, calls=%fused_computation.87 | convolution fusion | flops 1056966400 | bytes 25166272 | tf_op jit(solution)/shard_map/while/body/eval_jaxpr/nsb,nsjhd->bjhd/dot_general | solution.py:147
  782.5 6.5 reshape.376
  795.7 4.5 convolution_convert_fusion.4
  800.4 10.0 convolution_convert_fusion.1
  811.8 10.0 convolution_convert_fusion
  826.2 41.1 %all-reduce.1 = (f32[3]{0:T(128)S(1)}, f32[]{:T(128)}) all-reduce(f32[3]{0:T(128)S(1)} %pad_maximum_fusion.6, f32[]{:T(128)} %fusion.60), channel_id=1, replica_groups=mesh['rep'=8,'fsdp'=4] {'rep','fsdp'}, use_global_device_ids=true, to_apply=%region_42.45 | all-reduce | flops 4 | bytes 32 | tf_op jit(solution)/shard_map/psum | solution.py:235
  878.2 11.5 all-reduce
  894.7 48.0 %reduce-scatter.18.cloned.1.call-done = bf16[192,3072]{1,0:T(8,128)(2,1)} async-done(((bf16[768,3072]{1,0:T(8,128)(2,1)}), bf16[192,3072]{1,0:T(8,128)(2,1)}) %reduce-scatter.18.cloned.1.call-update) | async-done | bytes 1179664 | tf_op jit(solution)/shard_map/reduce_scatter | solution.py:304
  942.7 88.1 %reduce-scatter.20.cloned.1.call-done = bf16[768,768]{1,0:T(8,128)(2,1)} async-done(((bf16[3072,768]{1,0:T(8,128)(2,1)}), bf16[768,768]{1,0:T(8,128)(2,1)}) %reduce-scatter.20.cloned.1.call-update) | async-done | bytes 1179664 | tf_op jit(solution)/shard_map/reduce_scatter | solution.py:307
  1030.8 155.6 %all-reduce.4 = (f32[192,768]{0,1:T(8,128)S(1)}, f32[192,768]{0,1:T(8,128)S(1)}, f32[192,768]{0,1:T(8,128)S(1)}, f32[192,768]{1,0:T(8,128)}, f32[192,3072]{1,0:T...) all-reduce(bf16[192,768]{0,1:T(8,128)(2,1)S(1)} %copy.151, ...), channel_id=1, replica_groups=mesh['rep'=8,'fsdp'=4] {'rep'}, use_global_device_ids=true, to_apply=%region_15.18 | all-reduce | flops 1771776 | bytes 10632192 | tf_op jit(solution)/shard_map/psum | solution.py:317
  (301 shorter events, 109.6 us)
Async XLA Ops:
  7.2 5.7 copy-start.19
  7.2 44.5 %all-gather.11.cloned.1.call-start = ((), (), s32[]{:S(2)}) async-start(), calls=%async_computation.8 | async-start | bytes 1474560 | tf_op jit(solution)/shard_map/all_gather | solution.py:186
  7.9 66.1 %all-gather.13.cloned.1.call-start = ((), (), s32[]{:S(2)}) async-start(), calls=%async_computation.9 | async-start | bytes 1474560 | tf_op jit(solution)/shard_map/all_gather | solution.py:187
  8.7 96.5 %all-gather.9.cloned.1.call-start = ((), (), s32[]{:S(2)}) async-start(), calls=%async_computation.7 | async-start | bytes 1474560 | tf_op jit(solution)/shard_map/all_gather | solution.py:188
  9.4 293.1 %all-gather.15.cloned.1.call-start = ((), (), s32[]{:S(2)}) async-start(), calls=%async_computation.10 | async-start | bytes 1474560 | tf_op jit(solution)/shard_map/all_gather | solution.py:189
  10.0 298.5 %all-gather.17.cloned.1.call-start = ((), (), s32[]{:S(2)}) async-start(), calls=%async_computation.11 | async-start | bytes 5898240 | tf_op jit(solution)/shard_map/all_gather | solution.py:190
  10.6 20.9 %copy-start.71 = (bf16[8,192]{1,0:T(8,128)(2,1)S(1)}, bf16[8,192]{1,0:T(8,128)(2,1)}, u32[]{:S(2)}) copy-start(bf16[8,192]{1,0:T(8,128)(2,1)} %param.26) | copy-start | bytes 9220
  10.6 35.1 %slice-start.2 = ((s32[1024]{0:T(1024)}), s32[128]{0:T(128)S(1)}, s32[]{:S(2)}) async-start(s32[1024]{0:T(1024)} %param.17), calls=%async_computation.22 | async-start | bytes 1024 | tf_op jit(solution)/shard_map/while/body/eval_jaxpr/slice | solution.py:74
  10.6 336.3 %all-gather.19.cloned.1.call-start = ((), (), s32[]{:S(2)}) async-start(), calls=%async_computation.12 | async-start | bytes 5898240 | tf_op jit(solution)/shard_map/all_gather | solution.py:191
  11.2 879.1 %reduce-scatter.28.cloned.1.call-start = ((), (), s32[]{:S(2)}) async-start(), calls=%async_computation.19 | async-start | bytes 245760
  14.8 36.9 %copy-start.32 = (bf16[1024,768]{1,0:T(8,128)(2,1)S(1)}, bf16[1024,768]{1,0:T(8,128)(2,1)}, u32[]{:S(2)}) copy-start(bf16[1024,768]{1,0:T(8,128)(2,1)} %param.16) | copy-start | bytes 4718596
  45.9 76.7 %copy-start.24 = (pred[128,1024]{1,0:T(8,128)(4,1)}, pred[128,1024]{1,0:T(8,128)(4,1)S(1)}, u32[]{:S(2)}) copy-start(pred[128,1024]{1,0:T(8,128)(4,1)S(1)} %broadcast_compare_fusion) | copy-start | bytes 393220
  54.5 65.3 %copy-start.29 = (bf16[128,768]{0,1:T(8,128)(2,1)}, bf16[128,768]{0,1:T(8,128)(2,1)S(1)}, u32[]{:S(2)}) copy-start(bf16[128,768]{0,1:T(8,128)(2,1)S(1)} %slice.120) | copy-start | bytes 589828
  189.7 22.4 %copy-start.1 = (bf16[14,8,64,12,64]{4,2,3,1,0:T(8,128)(2,1)S(1)}, bf16[14,8,64,12,64]{4,2,3,1,0:T(8,128)(2,1)}, u32[]{:S(2)}) copy-start(bf16[14,8,64,12,64]{4,2,3,1,0:T(8,128)(2,1)} %get-tuple-element.155) | copy-start | bytes 33030148
  212.2 8.2 copy-start.2
  212.2 8.2 copy-start.4
  302.5 5.5 copy-start.77
  308.0 38.8 %copy-start.15 = (f32[1024,768]{0,1:T(8,128)}, f32[1024,768]{0,1:T(8,128)S(1)}, u32[]{:S(2)}) copy-start(f32[1024,768]{0,1:T(8,128)S(1)} %get-tuple-element.148) | copy-start | bytes 9437188
  308.1 87.2 %copy-start.52 = (f32[1024]{0:T(1024)}, f32[1024]{0:T(1024)S(1)}, u32[]{:S(2)}) copy-start(f32[1024]{0:T(1024)S(1)} %broadcast_multiply_fusion.1) | copy-start | bytes 12292
  308.5 86.8 %copy-start.56 = (f32[1024]{0:T(1024)}, f32[1024]{0:T(1024)S(1)}, u32[]{:S(2)}) copy-start(f32[1024]{0:T(1024)S(1)} %fusion.46) | copy-start | bytes 12292
  308.8 38.1 %copy-start.69 = (f32[768]{0:T(1024)S(1)}, f32[768]{0:T(1024)}, u32[]{:S(2)}) copy-start(f32[768]{0:T(1024)} %get-tuple-element.119) | copy-start | bytes 9220
  308.8 38.1 %copy-start.72 = (f32[1024]{0:T(1024)S(1)}, f32[1024]{0:T(1024)}, u32[]{:S(2)}) copy-start(f32[1024]{0:T(1024)} %compare_convert_fusion) | copy-start | bytes 12292
  346.9 13.4 %copy-start.12 = (bf16[1024,768]{0,1:T(8,128)(2,1)S(1)}, bf16[1024,768]{0,1:T(8,128)(2,1)}, u32[]{:S(2)}) copy-start(bf16[1024,768]{0,1:T(8,128)(2,1)} %copy.100) | copy-start | bytes 4718596
  346.9 13.4 %copy-start.49 = (f32[768]{0:T(1024)S(1)}, f32[768]{0:T(1024)}, u32[]{:S(2)}) copy-start(f32[768]{0:T(1024)} %get-tuple-element.117) | copy-start | bytes 9220
  365.2 18.1 %copy-start.35 = (bf16[1024,768]{0,1:T(8,128)(2,1)}, bf16[1024,768]{0,1:T(8,128)(2,1)S(1)}, u32[]{:S(2)}) copy-start(bf16[1024,768]{0,1:T(8,128)(2,1)S(1)} %get-tuple-element.138) | copy-start | bytes 4718596
  383.4 12.0 %copy-start.16 = (f32[1024,768]{0,1:T(8,128)S(1)}, f32[1024,768]{0,1:T(8,128)}, u32[]{:S(2)}) copy-start(f32[1024,768]{0,1:T(8,128)} %copy-done.15) | copy-start | bytes 9437188
  403.6 21.7 %copy-start.10 = (f32[12,64,1024]{2,1,0:T(8,128)}, f32[12,64,1024]{2,1,0:T(8,128)S(1)}, u32[]{:S(2)}) copy-start(f32[12,64,1024]{2,1,0:T(8,128)S(1)} %fusion.43) | copy-start | bytes 9437188
  416.1 7.3 copy-start.14
  429.0 7.7 copy-start.3
  429.0 7.7 copy-start.28
  573.7 49.0 %copy-start.46 = (s32[14,8]{0,1:T(8,128)S(1)}, s32[14,8]{0,1:T(8,128)}, u32[]{:S(2)}) copy-start(s32[14,8]{0,1:T(8,128)} %copy-done.45) | copy-start | bytes 1348
  622.7 30.8 %copy-start.59 = (bf16[1,768]{1,0:T(2,128)(2,1)S(1)}, bf16[1,768]{1,0:T(2,128)(2,1)}, u32[]{:S(2)}) copy-start(bf16[1,768]{1,0:T(2,128)(2,1)} %reshape.384) | copy-start | bytes 4612
  622.7 30.8 %copy-start.60 = (bf16[1,768]{1,0:T(2,128)(2,1)S(1)}, bf16[1,768]{1,0:T(2,128)(2,1)}, u32[]{:S(2)}) copy-start(bf16[1,768]{1,0:T(2,128)(2,1)} %reshape.383) | copy-start | bytes 4612
  622.7 30.8 %copy-start.61 = (bf16[1,768]{1,0:T(2,128)(2,1)S(1)}, bf16[1,768]{1,0:T(2,128)(2,1)}, u32[]{:S(2)}) copy-start(bf16[1,768]{1,0:T(2,128)(2,1)} %reshape.381) | copy-start | bytes 4612
  622.7 30.8 %copy-start.62 = (bf16[1,768]{1,0:T(2,128)(2,1)S(1)}, bf16[1,768]{1,0:T(2,128)(2,1)}, u32[]{:S(2)}) copy-start(bf16[1,768]{1,0:T(2,128)(2,1)} %stack.92) | copy-start | bytes 4612
  622.7 30.8 %copy-start.63 = (bf16[1,768]{1,0:T(2,128)(2,1)S(1)}, bf16[1,768]{1,0:T(2,128)(2,1)}, u32[]{:S(2)}) copy-start(bf16[1,768]{1,0:T(2,128)(2,1)} %reshape.382) | copy-start | bytes 4612
  622.7 30.8 %copy-start.64 = (bf16[1,768]{1,0:T(2,128)(2,1)S(1)}, bf16[1,768]{1,0:T(2,128)(2,1)}, u32[]{:S(2)}) copy-start(bf16[1,768]{1,0:T(2,128)(2,1)} %stack.91) | copy-start | bytes 4612
  654.4 236.8 %reduce-scatter.22.cloned.1.call-start = ((), (), s32[]{:S(2)}) async-start(), calls=%async_computation.16 | async-start | bytes 1474560
  662.2 6.5 copy-start.11
  681.1 211.3 %reduce-scatter.26.cloned.1.call-start = ((), (), s32[]{:S(2)}) async-start(), calls=%async_computation.18 | async-start | bytes 1474560
  752.1 141.4 %reduce-scatter.24.cloned.1.call-start = ((), (), s32[]{:S(2)}) async-start(), calls=%async_computation.17 | async-start | bytes 1474560
  782.5 6.5 copy-start.9
  782.5 6.5 copy-start.30
  795.7 99.0 %reduce-scatter.16.cloned.1.call-start = ((), (), s32[]{:S(2)}) async-start(), calls=%async_computation.13 | async-start | bytes 1474560 | tf_op jit(solution)/shard_map/reduce_scatter | solution.py:301
  800.3 142.4 %reduce-scatter.18.cloned.1.call-start = ((), (), s32[]{:S(2)}) async-start(), calls=%async_computation.14 | async-start | bytes 5898240 | tf_op jit(solution)/shard_map/reduce_scatter | solution.py:304
  810.4 220.4 %reduce-scatter.20.cloned.1.call-start = ((), (), s32[]{:S(2)}) async-start(), calls=%async_computation.15 | async-start | bytes 5898240 | tf_op jit(solution)/shard_map/reduce_scatter | solution.py:307
  821.7 45.6 %copy-start.20 = (bf16[1024,768]{0,1:T(8,128)(2,1)S(1)}, bf16[1024,768]{0,1:T(8,128)(2,1)}, u32[]{:S(2)}) copy-start(bf16[1024,768]{0,1:T(8,128)(2,1)} %get-tuple-element.149) | copy-start | bytes 4718596
  821.8 47.1 %copy-start.40 = (bf16[896,768]{0,1:T(8,128)(2,1)S(1)}, bf16[896,768]{0,1:T(8,128)(2,1)}, u32[]{:S(2)}) copy-start(bf16[896,768]{0,1:T(8,128)(2,1)} %reshape.375) | copy-start | bytes 4128772
  (47 other events, 120.3 us)
Sparse Core Ops, SparseCore 0:
  9.6 33.3 all-gather.10
  44.5 29.5 all-gather.12
  75.7 29.4 all-gather.8
  106.6 29.4 all-gather.14
  137.6 88.6 all-gather.16
  227.6 87.7 all-gather.18
  654.5 19.3 reduce-scatter.27
  681.2 29.0 reduce-scatter.21
  752.2 29.0 reduce-scatter.25
  795.7 29.0 reduce-scatter.23
  827.1 28.7 reduce-scatter.15
  858.1 84.5 reduce-scatter.17
  945.0 85.7 reduce-scatter.19
where the time goes:
time: 1200 us
  matrix products  377 us (31%)
  local copies, waits for them, and re-layouts  278 us (23%)
  blocking collectives  237 us (20%)
  waiting for transfers between devices  176 us (15%)
  other arithmetic  112 us (9%)
  between operations  16.4 us (1%)
    psum x1, blocking collectives, per_device(): lax.psum((shard_sums[0], shard_sums[1], shard_sums[2], shard_sums[3], sha...  156 us
    reduce_scatter x1, waiting for transfers between devices, per_device(): lax.psum_scatter(grad_down.astype(jnp.bfloat16), 'fsdp', scatter_dimensio...  88.1 us
    unnamed x2, matrix products  62.3 us
    transpose x1, local copies, waits for them, and re-layouts, attend_backward(): jnp.einsum('nhqsj,nqhd->nsjhd', probs_low, d_heads[2:], preferred_element...  49 us
    mul x1, local copies, waits for them, and re-layouts, attend_backward(): 0.125 * jnp.einsum('nhqsj,nqhd->nsjhd', d_scores, q_heads[2:], preferred_...  49 us
    reduce_scatter x1, waiting for transfers between devices, per_device(): lax.psum_scatter(grad_up.astype(jnp.bfloat16), 'fsdp', scatter_dimension=...  48 us
    psum x1, blocking collectives, per_device(): squares, counted = lax.psum((squares, jnp.sum(valid)), ('rep', 'fsdp'))  41.1 us
    dot_general x1, matrix products, per_device(): jnp.dot(normed_low, full_up, preferred_element_type=jnp.float32)  38.1 us
  transfers between devices with their start and end apart: 13, of which 4 were waited for; matrix products, arithmetic and copies ran while one was open for 37% of the time, Pallas kernels for 0%

commit v1 on v0

v1 whole, which is shorter than its diff:
```python
import jax
import jax.numpy as jnp
from jax import lax
from jax.experimental import pallas as pl
from jax.experimental.pallas import tpu as pltpu
from jax.sharding import PartitionSpec as P

D = 768
H = 12
DH = 64
BLK = 64
SEQ_LEN = 1024
NB = 16


masked_score = -1e30
layer_eps = 1e-05


def normalize(values, gain, shift):
    centered = values - jnp.mean(values, axis=-1, keepdims=True)
    variance = jnp.mean(centered * centered, axis=-1, keepdims=True)
    return centered * lax.rsqrt(variance + layer_eps) * gain + shift


def gelu_exact(values):
    return jax.nn.gelu(values, approximate=False)


def dot_tn(left, right):
    return lax.dot_general(
        left, right, (((0,), (0,)), ((), ())), preferred_element_type=jnp.float32
    )


def dot_nt(left, right):
    return lax.dot_general(
        left, right, (((1,), (1,)), ((), ())), preferred_element_type=jnp.float32
    )


def col_sums(values):
    return jnp.sum(values.astype(jnp.float32), axis=0)


LOG2E=1.4426950408889634
BIG=1e30

def dot_nn(a,b): return lax.dot_general(a,b,(((1,),(0,)),((),())),preferred_element_type=jnp.float32)

def mask_features(seg_row, random_row):
    blocks = jnp.arange(NB, dtype=jnp.int32)
    near = jnp.abs(blocks[:, None] - blocks[None, :]) <= 1
    first = (blocks[:, None] < 2) | (blocks[None, :] < 2)
    picked = jnp.any(random_row[:, :, None] == blocks[None, None, :], axis=1)
    seen = first | near | picked
    q_block = jnp.where(seen, 0.0, -BIG)
    q_block = jnp.repeat(q_block, BLK, axis=0)
    k_block = jnp.repeat(jnp.eye(NB, dtype=jnp.float32), BLK, axis=0)
    numbers = jnp.arange(-1, 2, dtype=jnp.int32)
    same = seg_row[:, None] == numbers[None, :]
    q_seg = jnp.where(same, 0.0, -BIG)
    k_seg = same.astype(jnp.float32)
    rest = SEQ_LEN, 128 - NB - 3
    ones = jnp.ones((SEQ_LEN, 3), jnp.float32)
    q_feat = jnp.concatenate([q_block, q_seg, jnp.zeros(rest, jnp.float32)], axis=1)
    k_feat = jnp.concatenate([k_block, k_seg, ones, jnp.zeros((SEQ_LEN, 128 - NB - 6), jnp.float32)], axis=1)
    return q_feat.astype(jnp.bfloat16), k_feat.astype(jnp.bfloat16)

TQ=256
def fwd_kernel(q_ref,k_ref,v_ref,qf_ref,kf_ref,o_ref,aux_ref,qc,kc,vm):
    lane = lax.broadcasted_iota(jnp.int32,(SEQ_LEN,128),1)
    kc[:,:128]=k_ref[...]
    kc[:,128:]=kf_ref[...]
    q=q_ref[...]*jnp.bfloat16(0.125)
    v=v_ref[...]
    zero=jnp.zeros_like(q)
    for h in range(2):
        sel = (lane<64) if h==0 else (lane>=64)
        qc[h,:,:128]=jnp.where(sel,q,zero)
        qc[h,:,128:]=qf_ref[...]
        vm[h]=jnp.where(sel,v,zero)
    for t in range(SEQ_LEN//TQ):
        rows=pl.ds(t*TQ,TQ)
        total=None
        for h in range(2):
            s=dot_nt(qc[h,rows,:],kc[...])
            m=jnp.max(s,axis=1,keepdims=True)
            p=jnp.exp2((s-m)*LOG2E)
            l=jnp.sum(p,axis=1,keepdims=True)
            o=dot_nn(p.astype(jnp.bfloat16),vm[h])*(1.0/l)
            total=o if total is None else total+o
            lse=-(m+jnp.log(l))
            hi=lse.astype(jnp.bfloat16).astype(jnp.float32)
            r=lse-hi
            mid=r.astype(jnp.bfloat16).astype(jnp.float32)
            lo=r-mid
            ln=lax.broadcasted_iota(jnp.int32,(TQ,128),1)
            a=jnp.where(ln==19,hi,jnp.where(ln==20,mid,jnp.where(ln==21,lo,qf_ref[rows,:].astype(jnp.float32))))
            aux_ref[h,rows,:]=a.astype(jnp.bfloat16)
        o_ref[rows,:]=total.astype(jnp.bfloat16)

def attention_forward(q,k,v,qf,kf):
    pair=pl.BlockSpec((SEQ_LEN,128),lambda i:(0,i))
    whole=pl.BlockSpec((SEQ_LEN,128),lambda i:(0,0))
    return pl.pallas_call(fwd_kernel,grid=(H//2,),
        in_specs=[pair,pair,pair,whole,whole],
        out_specs=[pair,pl.BlockSpec((2,SEQ_LEN,128),lambda i:(i,0,0))],
        out_shape=[jax.ShapeDtypeStruct((SEQ_LEN,D),jnp.bfloat16),jax.ShapeDtypeStruct((H,SEQ_LEN,128),jnp.bfloat16)],
        scratch_shapes=[pltpu.VMEM((2,SEQ_LEN,256),jnp.bfloat16),pltpu.VMEM((SEQ_LEN,256),jnp.bfloat16),pltpu.VMEM((2,SEQ_LEN,128),jnp.bfloat16)],
        compiler_params=pltpu.CompilerParams(vmem_limit_bytes=48<<20),
        name="attention_forward")(q,k,v,qf,kf)

TK=256
def bwd_kernel(q_ref,k_ref,v_ref,do_ref,o_ref,aux_ref,kf_ref,dq_ref,dk_ref,dv_ref,qc,dc,kc,vc,km,dqa):
    lane = lax.broadcasted_iota(jnp.int32,(SEQ_LEN,128),1)
    kc[:,:128]=k_ref[...]
    kc[:,128:]=kf_ref[...]
    vc[:,:128]=v_ref[...]
    vc[:,128:]=kf_ref[...]
    q=q_ref[...]*jnp.bfloat16(0.125)
    k=k_ref[...]*jnp.bfloat16(0.125)
    do=do_ref[...]
    prod=do.astype(jnp.float32)*o_ref[...].astype(jnp.float32)
    zero=jnp.zeros_like(q)
    for h in range(2):
        sel = (lane<64) if h==0 else (lane>=64)
        qc[h,:,:128]=jnp.where(sel,q,zero)
        qc[h,:,128:]=aux_ref[h]
        km[h]=jnp.where(sel,k,zero)
        dc[h,:,:128]=jnp.where(sel,do,zero)
        delta=-jnp.sum(jnp.where(sel,prod,0.0),axis=1,keepdims=True)
        hi=delta.astype(jnp.bfloat16).astype(jnp.float32)
        lo=delta-hi
        dc[h,:,128:]=jnp.where(lane==19,hi,jnp.where(lane==20,lo,0.0)).astype(jnp.bfloat16)
    for t in range(SEQ_LEN//TK):
        rows=pl.ds(t*TK,TK)
        dv=None;dk=None;dq=None
        for h in range(2):
            s=dot_nt(kc[rows,:],qc[h])
            p=jnp.exp2(s*LOG2E)
            dp=dot_nt(vc[rows,:],dc[h])
            ds=(p*dp).astype(jnp.bfloat16)
            pb=p.astype(jnp.bfloat16)
            dvh=dot_nn(pb,dc[h,:,:128])
            dkh=dot_nn(ds,qc[h,:,:128])
            dqh=dot_tn(ds,km[h,rows,:])
            dv=dvh if dv is None else dv+dvh
            dk=dkh if dk is None else dk+dkh
            dq=dqh if dq is None else dq+dqh
        dk_ref[rows,:]=dk.astype(jnp.bfloat16)
        dv_ref[rows,:]=dv.astype(jnp.bfloat16)
        if t==0: dqa[...]=dq
        else: dqa[...]+=dq
    dq_ref[...]=dqa[...].astype(jnp.bfloat16)

def attention_backward(q,k,v,do,o,aux,kf):
    pair=pl.BlockSpec((SEQ_LEN,128),lambda i:(0,i))
    whole=pl.BlockSpec((SEQ_LEN,128),lambda i:(0,0))
    sd=jax.ShapeDtypeStruct((SEQ_LEN,D),jnp.bfloat16)
    B=jnp.bfloat16
    return pl.pallas_call(bwd_kernel,grid=(H//2,),
        in_specs=[pair]*5+[pl.BlockSpec((2,SEQ_LEN,128),lambda i:(i,0,0)),whole],
        out_specs=[pair]*3,out_shape=[sd]*3,
        scratch_shapes=[pltpu.VMEM((2,SEQ_LEN,256),B),pltpu.VMEM((2,SEQ_LEN,256),B),pltpu.VMEM((SEQ_LEN,256),B),pltpu.VMEM((SEQ_LEN,256),B),pltpu.VMEM((2,SEQ_LEN,128),B),pltpu.VMEM((SEQ_LEN,128),jnp.float32)],
        compiler_params=pltpu.CompilerParams(vmem_limit_bytes=48<<20),
        name="attention_backward")(q,k,v,do,o,aux,kf)


def per_device(
    tokens,
    segments,
    random_blocks,
    out_grad,
    w_query,
    w_key,
    w_value,
    w_out,
    w_up,
    w_down,
    vectors,
    up_bias,
):
    gathered = (
        lax.all_gather(w_query, "fsdp", axis=0, tiled=True),
        lax.all_gather(w_key, "fsdp", axis=0, tiled=True),
        lax.all_gather(w_value, "fsdp", axis=0, tiled=True),
        lax.all_gather(w_out, "fsdp", axis=0, tiled=True),
        lax.all_gather(w_up, "fsdp", axis=0, tiled=True),
        lax.all_gather(w_down, "fsdp", axis=0, tiled=True),
        lax.all_gather(vectors, "fsdp", axis=1, tiled=True),
        lax.all_gather(up_bias, "fsdp", axis=0, tiled=True),
    )
    full_query, full_key, full_value, full_out, full_up, full_down, full_vectors, full_upbias = (
        gathered
    )
    vec_float = full_vectors.astype(jnp.float32)
    inputs = tokens.astype(jnp.float32)
    q_low = (jnp.dot(tokens, full_query, preferred_element_type=jnp.float32) + vec_float[0]).astype(
        jnp.bfloat16
    )
    k_low = jnp.dot(tokens, full_key, preferred_element_type=jnp.float32).astype(jnp.bfloat16)
    v_low = (jnp.dot(tokens, full_value, preferred_element_type=jnp.float32) + vec_float[1]).astype(
        jnp.bfloat16
    )
    q_feat, k_feat = mask_features(segments, random_blocks[0])
    mixed_low, aux = attention_forward(q_low, k_low, v_low, q_feat, k_feat)
    attn_out = jnp.dot(mixed_low, full_out, preferred_element_type=jnp.float32) + vec_float[2]
    first_sum = inputs + attn_out
    normed_one, pull_one = jax.vjp(normalize, first_sum, vec_float[3], vec_float[4])
    normed_low = normed_one.astype(jnp.bfloat16)
    up_proj = jnp.dot(normed_low, full_up, preferred_element_type=jnp.float32) + full_upbias.astype(
        jnp.float32
    )
    activated, pull_gelu = jax.vjp(gelu_exact, up_proj)
    activated_low = activated.astype(jnp.bfloat16)
    mlp_out = jnp.dot(activated_low, full_down, preferred_element_type=jnp.float32) + vec_float[5]
    second_sum = normed_one + mlp_out
    layer_out, pull_two = jax.vjp(normalize, second_sum, vec_float[6], vec_float[7])
    valid = (segments >= 0).astype(jnp.float32)[:, None]
    squares = jnp.stack(
        [
            jnp.sum(valid * first_sum * first_sum),
            jnp.sum(valid * attn_out * attn_out),
            jnp.sum(valid * mlp_out * mlp_out),
        ]
    )
    squares, counted = lax.psum((squares, jnp.sum(valid)), ("rep", "fsdp"))
    rms_values = jnp.sqrt(squares / (counted * D))
    regathered = (
        lax.all_gather(w_query, "fsdp", axis=0, tiled=True),
        lax.all_gather(w_key, "fsdp", axis=0, tiled=True),
        lax.all_gather(w_value, "fsdp", axis=0, tiled=True),
        lax.all_gather(w_out, "fsdp", axis=0, tiled=True),
        lax.all_gather(w_up, "fsdp", axis=0, tiled=True),
        lax.all_gather(w_down, "fsdp", axis=0, tiled=True),
    )
    back_query, back_key, back_value, back_out, back_up, back_down = regathered
    d_second, d_gain_two, d_shift_two = pull_two(out_grad.astype(jnp.float32))
    d_mlp = d_second.astype(jnp.bfloat16)
    d_up = pull_gelu(dot_nt(d_mlp, back_down))[0].astype(jnp.bfloat16)
    d_normed = d_second + dot_nt(d_up, back_up)
    d_first, d_gain_one, d_shift_one = pull_one(d_normed)
    d_attn = d_first.astype(jnp.bfloat16)
    d_mixed = dot_nt(d_attn, back_out).astype(jnp.bfloat16)
    dq_low, dk_low, dv_low = attention_backward(
        q_low, k_low, v_low, d_mixed, mixed_low, aux, k_feat
    )
    tokens_grad = (
        d_first + dot_nt(dq_low, back_query) + dot_nt(dk_low, back_key) + dot_nt(dv_low, back_value)
    )
    grad_query = dot_tn(tokens, dq_low)
    grad_key = dot_tn(tokens, dk_low)
    grad_value = dot_tn(tokens, dv_low)
    grad_out = dot_tn(mixed_low, d_attn)
    grad_up = dot_tn(normed_low, d_up)
    grad_down = dot_tn(activated_low, d_mlp)
    grad_vectors = jnp.stack(
        [
            col_sums(dq_low),
            col_sums(dv_low),
            col_sums(d_attn),
            d_gain_one,
            d_shift_one,
            col_sums(d_mlp),
            d_gain_two,
            d_shift_two,
        ]
    )
    grad_upbias = col_sums(d_up)
    shard_sums = (
        lax.psum_scatter(
            grad_query.astype(jnp.bfloat16), "fsdp", scatter_dimension=0, tiled=True
        ).astype(jnp.float32),
        lax.psum_scatter(
            grad_key.astype(jnp.bfloat16), "fsdp", scatter_dimension=0, tiled=True
        ).astype(jnp.float32),
        lax.psum_scatter(
            grad_value.astype(jnp.bfloat16), "fsdp", scatter_dimension=0, tiled=True
        ).astype(jnp.float32),
        lax.psum_scatter(
            grad_out.astype(jnp.bfloat16), "fsdp", scatter_dimension=0, tiled=True
        ).astype(jnp.float32),
        lax.psum_scatter(
            grad_up.astype(jnp.bfloat16), "fsdp", scatter_dimension=0, tiled=True
        ).astype(jnp.float32),
        lax.psum_scatter(
            grad_down.astype(jnp.bfloat16), "fsdp", scatter_dimension=0, tiled=True
        ).astype(jnp.float32),
        lax.psum_scatter(
            grad_vectors.astype(jnp.bfloat16), "fsdp", scatter_dimension=1, tiled=True
        ).astype(jnp.float32),
        lax.psum_scatter(
            grad_upbias.astype(jnp.bfloat16), "fsdp", scatter_dimension=0, tiled=True
        ).astype(jnp.float32),
    )
    results = lax.psum(
        (
            shard_sums[0],
            shard_sums[1],
            shard_sums[2],
            shard_sums[3],
            shard_sums[4],
            shard_sums[5],
            shard_sums[6],
            shard_sums[7],
        ),
        "rep",
    )
    return (
        layer_out.astype(jnp.bfloat16),
        tokens_grad.astype(jnp.bfloat16),
        results[0],
        results[1],
        results[2],
        results[3],
        results[4],
        results[5],
        results[6],
        results[7],
        rms_values,
    )


def solution(mesh):
    in_specs = (
        P(("rep", "fsdp"), None),
        P(("rep", "fsdp")),
        P(("rep", "fsdp"), None, None),
        P(("rep", "fsdp"), None),
        P("fsdp", None),
        P("fsdp", None),
        P("fsdp", None),
        P("fsdp", None),
        P("fsdp", None),
        P("fsdp", None),
        P(None, "fsdp"),
        P("fsdp"),
    )
    out_specs = (
        P(("rep", "fsdp"), None),
        P(("rep", "fsdp"), None),
        P("fsdp", None),
        P("fsdp", None),
        P("fsdp", None),
        P("fsdp", None),
        P("fsdp", None),
        P("fsdp", None),
        P(None, "fsdp"),
        P("fsdp"),
        P(),
    )
    return jax.shard_map(
        per_device, mesh=mesh, in_specs=in_specs, out_specs=out_specs, check_vma=False
    )
```

time: 1200 us -> 903 us (0.75)
  local copies, waits for them, and re-layouts: 278 us -> 31 us
  matrix products: 377 us -> 138 us
  waiting for transfers between devices: 176 us -> 388 us
  other arithmetic: 112 us -> 12.9 us
  Pallas kernels: 0 us -> 70.6 us
    dot_general x12 -> x0, matrix products: 180 us -> none  [the longest x1 37.6 us: attend_backward(): jnp.einsum('nhqsj,nqhd->nsjhd', probs_low, d_heads[2:], preferred_element...]
    all_gather x1, waiting for transfers between devices: 0.02 us -> 79.5 us  [per_device(): lax.all_gather(w_up, 'fsdp', axis=0, tiled=True)]
    pallas_call x0 -> x2, Pallas kernels: none -> 70.6 us  [the longest x1 40.7 us: attention_backward(): pl.pallas_call(bwd_kernel, grid=(H // 2,), in_specs=[pair] * 5 + [pl.Bloc...]
    unnamed x2 -> x0, matrix products: 62.3 us -> none
    mul x2 -> x0, local copies, waits for them, and re-layouts: 53.1 us -> none  [the longest x1 49 us: attend_backward(): 0.125 * jnp.einsum('nhqsj,nqhd->nsjhd', d_scores, q_heads[2:], preferred_...]
    transpose x2 -> x0, local copies, waits for them, and re-layouts: 52.9 us -> none  [the longest x1 49 us: attend_backward(): jnp.einsum('nhqsj,nqhd->nsjhd', probs_low, d_heads[2:], preferred_element...]
    all_gather x1, waiting for transfers between devices: 0.02 us -> 51.2 us  [per_device(): lax.all_gather(w_down, 'fsdp', axis=0, tiled=True)]
    reshape x11 -> x0, local copies, waits for them, and re-layouts: 48 us -> none  [the longest x3 17.9 us: attend_backward(): d_value = dv_blocks.reshape(SEQ_LEN, D) + dv_glob.reshape(SEQ_LEN, D)]
  transfers between devices with their start and end apart: 13 -> 13, of which waited for: 4 -> 7; matrix products, arithmetic and copies ran while one was open for 37% -> 13% of each run, Pallas kernels for 0% -> 3%
where the time goes in v1:
time: 903 us; the launch traced here: 893 us
  waiting for transfers between devices  388 us (43%)
  blocking collectives  237 us (26%)
  matrix products  138 us (15%)
  Pallas kernels  70.6 us (8%)
  local copies, waits for them, and re-layouts  31 us (3%)
  between operations  16.1 us (2%)
  other arithmetic  12.9 us (1%)
    psum x1, blocking collectives, per_device(): lax.psum((shard_sums[0], shard_sums[1], shard_sums[2], shard_sums[3], sha...  156 us
    reduce_scatter x1, waiting for transfers between devices, per_device(): lax.psum_scatter(grad_up.astype(jnp.bfloat16), 'fsdp', scatter_dimension=...  88.1 us
    reduce_scatter x1, waiting for transfers between devices, per_device(): lax.psum_scatter(grad_down.astype(jnp.bfloat16), 'fsdp', scatter_dimensio...  86.1 us
    all_gather x1, waiting for transfers between devices, per_device(): lax.all_gather(w_up, 'fsdp', axis=0, tiled=True)  79.5 us
    all_gather x1, waiting for transfers between devices, per_device(): lax.all_gather(w_down, 'fsdp', axis=0, tiled=True)  51.2 us
    psum x1, blocking collectives, per_device(): squares, counted = lax.psum((squares, jnp.sum(valid)), ('rep', 'fsdp'))  40.8 us
    pallas_call x1, Pallas kernels, attention_backward(): pl.pallas_call(bwd_kernel, grid=(H // 2,), in_specs=[pair] * 5 + [pl.Bloc...  40.7 us
    dot_general x1, matrix products, per_device(): jnp.dot(normed_low, full_up, preferred_element_type=jnp.float32)  38 us
  transfers between devices with their start and end apart: 13, of which 7 were waited for; matrix products, arithmetic and copies ran while one was open for 13% of the time, Pallas kernels for 3%

profile of v1, /device:TPU:0, one launch (start us, length us, event | category | flops | bytes accessed | tf_op | source)
XLA Modules:
  0.0 893.0 jit_solution(8768370067927201646)
XLA Ops:
  12.4 15.1 %all-gather = bf16[4,192,8]{1,2,0:T(8,128)(2,1)S(1)} all-gather(bf16[1,192,8]{1,2,0:T(8,128)(2,1)S(1)} %bitcast.69), channel_id=1, replica_groups=mesh['rep'=8,'fsdp'=4] {'fsdp'}, dimensions={0}, use_global_device_ids=true | all-gather | bytes 15360 | tf_op jit(solution)/shard_map/all_gather | solution.py:191
  27.6 1.6 copy.63
  29.9 1.6 copy.61
  31.5 13.4 %all-gather.1 = bf16[4,1,768]{2,1,0:T(2,128)(2,1)S(1)} all-gather(bf16[1,1,768]{2,1,0:T(2,128)(2,1)S(1)} %reshape.124), channel_id=1, replica_groups=mesh['rep'=8,'fsdp'=4] {'fsdp'}, dimensions={0}, use_global_device_ids=true | all-gather | bytes 7680 | tf_op jit(solution)/shard_map/all_gather | solution.py:192
  46.8 2.7 convolution_convert_fusion.3.k_ref
  49.5 24.5 %all-gather.13.cloned.1.call-done = bf16[768,768]{1,0:T(8,128)(2,1)} async-done(((bf16[192,768]{1,0:T(8,128)(2,1)}), bf16[768,768]{1,0:T(8,128)(2,1)}) %all-gather.13.cloned.1.call-update) | async-done | bytes 1179664 | tf_op jit(solution)/shard_map/all_gather | solution.py:187
  74.0 3.8 add_convert_fusion.3.v_ref
  77.8 27.3 %all-gather.9.cloned.1.call-done = bf16[768,768]{1,0:T(8,128)(2,1)} async-done(((bf16[192,768]{1,0:T(8,128)(2,1)}), bf16[768,768]{1,0:T(8,128)(2,1)}) %all-gather.9.cloned.1.call-update) | async-done | bytes 1179664 | tf_op jit(solution)/shard_map/all_gather | solution.py:185
  105.1 2.7 add_convert_fusion.4.q_ref
  107.8 29.9 %attention_forward.1 = (bf16[1024,768]{1,0:T(8,128)(2,1)S(1)}, bf16[12,1024,128]{2,1,0:T(8,128)(2,1)}) custom-call(bf16[1024,768]{1,0:T(8,128)(2,1)S(1)} %add_convert_fusion.4.q_ref, bf16[1024,768]{1,0:T(8,128)(2,1)S(1)} %convolution_convert_fusion.3.k_ref, bf16[1024,768]{1,0:T(8,128)(2,1)} %add_convert_fusion.3.v_ref, bf16[1024,128]{1,0:T(8,128)(2,1)S(1)} %copy-done.6, ...), custom_call_target="tpu_custom_call" | custom-call | tf_op jit(solution)/shard_map/attention_forward/pallas_call | solution.py:106
  137.7 1.1 copy-done.1
  138.8 5.7 fusion.34
  144.5 1.6 copy-done.9
  146.5 79.5 %all-gather.17.cloned.1.call-done = bf16[768,3072]{1,0:T(8,128)(2,1)} async-done(((bf16[192,3072]{1,0:T(8,128)(2,1)}), bf16[768,3072]{1,0:T(8,128)(2,1)}) %all-gather.17.cloned.1.call-update) | async-done | bytes 4718608 | tf_op jit(solution)/shard_map/all_gather | solution.py:189
  226.1 38.0 %multiply_convert_fusion = (bf16[1024,3072]{1,0:T(8,128)(2,1)}, f32[1024,3072]{1,0:T(8,128)}, f32[1024,3072]{1,0:T(8,128)}) fusion(f32[3072]{0:T(1024)S(1)} %bitcast.66, bf16[768,3072]{1,0:T(8,128)(2,1)} %all-gather.17.cloned.1.call-done, f32[1024,768]{0,1:T(8,128)} %copy-done.9, f32[768]{0:T(1024)S(1)} %get-tuple-element.76, ...), kind=kOutput, calls=%fused_computation.3 | convolution fusion | flops 5043388416 | bytes 39348224 | tf_op jit(solution)/shard_map/dot_general | solution.py:212
  264.1 51.2 %all-gather.19.cloned.1.call-done = bf16[3072,768]{1,0:T(8,128)(2,1)} async-done(((bf16[768,768]{1,0:T(8,128)(2,1)}), bf16[3072,768]{1,0:T(8,128)(2,1)}) %all-gather.19.cloned.1.call-update) | async-done | bytes 4718608 | tf_op jit(solution)/shard_map/all_gather | solution.py:190
  315.4 13.4 %fusion.11 = (f32[]{:T(128)}, f32[]{:T(128)}, f32[1024]{0:T(1024)S(1)}, f32[1024,768]{0,1:T(8,128)S(1)}) fusion(f32[1024,768]{0,1:T(8,128)} %get-tuple-element.110, f32[1024]{0:T(1024)S(1)} %compare_convert_fusion.1, f32[768]{0:T(1024)S(1)} %get-tuple-element.78, f32[768]{0:T(1024)S(1)} %get-tuple-element.75, f32[768]{0:T(1024)S(1)} %get-tuple-element.76, ...), kind=kOutput, calls=%fused_computation.31 | convolution fusion | flops 4842847232 | bytes 20475912 | tf_op jit(solution)/shard_map/dot_general | solution.py:217
  329.5 2.9 fusion.9
  332.4 1.3 fusion.29
  333.6 17.6 %fusion.35 = (bf16[3072]{0:T(1024)(128)(2,1)S(1)}, bf16[1024,3072]{1,0:T(8,128)(2,1)}) fusion(f32[1024,3072]{1,0:T(8,128)} %get-tuple-element.102, bf16[1024,768]{0,1:T(8,128)(2,1)S(1)} %get-tuple-element.94, bf16[3072,768]{1,0:T(8,128)(2,1)} %all-gather.19.cloned.1.call-done, f32[1024,3072]{1,0:T(8,128)} %get-tuple-element.111, f32[3072]{0:T(1024)S(1)} %bitcast.67), kind=kOutput, calls=%fused_computation.104 | convolution fusion | flops 4882166784 | bytes 37767168 | tf_op jit(solution)/shard_map/dot_general | solution.py:37
  351.2 11.9 %multiply_reduce_fusion = (bf16[768]{0:T(1024)(128)(2,1)S(1)}, f32[1024]{0:T(1024)S(1)}, f32[]{:T(128)}, bf16[768]{0:T(1024)(128)(2,1)S(1)}, f32[1024,768]{0,1:T(8,128)S(1)}) fusion(f32[1024,768]{0,1:T(8,128)} %copy-done.9, f32[1024]{0:T(1024)S(1)} %fusion.22, f32[1024]{0:T(1024)S(1)} %broadcast_multiply_fusion.1, f32[768]{0:T(1024)S(1)} %get-tuple-element.77, ...), kind=kOutput, calls=%fused_computation.33 | convolution fusion | flops 4847563776 | bytes 22062084 | tf_op jit(solution)/shard_map/dot_general | solution.py:37
  364.3 1.8 copy-done.21
  366.1 2.6 convolution_convert_fusion.2.do_ref
  368.7 40.7 %attention_backward.1 = (bf16[1024,768]{1,0:T(8,128)(2,1)S(1)}, bf16[1024,768]{1,0:T(8,128)(2,1)S(1)}, bf16[1024,768]{1,0:T(8,128)(2,1)S(1)}) custom-call(bf16[1024,768]{1,0:T(8,128)(2,1)} %copy-done.1, bf16[1024,768]{1,0:T(8,128)(2,1)} %copy-done, bf16[1024,768]{1,0:T(8,128)(2,1)} %add_convert_fusion.3.v_ref, ...), custom_call_target="tpu_custom_call" | custom-call | tf_op jit(solution)/shard_map/attention_backward/pallas_call | solution.py:162
  409.4 1.1 copy-done.7
  412.2 3.9 fusion.14
  416.1 2.4 copy.77
  418.5 4.3 fusion.15
  422.8 2.5 copy.79
  425.7 2.5 fusion.16
  428.1 2.5 copy.81
  430.7 3.9 convolution_convert_fusion.4
  434.6 9.2 %convolution_convert_fusion = bf16[3072,768]{1,0:T(8,128)(2,1)} fusion(bf16[1024,3072]{1,0:T(8,128)(2,1)} %get-tuple-element.101, bf16[1024,768]{0,1:T(8,128)(2,1)} %copy-done.19), kind=kOutput, calls=%fused_computation.17 | convolution fusion | flops 4834197504 | bytes 12582912 | tf_op jit(solution)/shard_map/dot_general | solution.py:31
  443.9 9.9 %convolution_convert_fusion.1 = bf16[768,3072]{1,0:T(8,128)(2,1)} fusion(bf16[1024,3072]{1,0:T(8,128)(2,1)} %get-tuple-element.114, f32[1024,768]{0,1:T(8,128)} %copy-done.9, f32[768]{0:T(1024)S(1)} %get-tuple-element.76, f32[768]{0:T(1024)S(1)} %get-tuple-element.77, f32[1024]{0:T(1024)S(1)} %fusion.22, f32[1024]{0:T(1024)S(1)} %broadcast_multiply_fusion.1), kind=kOutput, calls=%fused_computation.18 | convolution fusion | flops 4838129664 | bytes 14170112 | tf_op jit(solution)/shard_map/dot_general | solution.py:31
  455.6 2.0 pad_maximum_fusion
  458.3 40.8 %all-reduce.1 = (f32[3]{0:T(128)S(1)}, f32[]{:T(128)}) all-reduce(f32[3]{0:T(128)S(1)} %pad_maximum_fusion, f32[]{:T(128)} %fusion.24), channel_id=1, replica_groups=mesh['rep'=8,'fsdp'=4] {'rep','fsdp'}, use_global_device_ids=true, to_apply=%region_37.38 | all-reduce | flops 4 | bytes 32 | tf_op jit(solution)/shard_map/psum | solution.py:228
  499.1 2.8 fusion.36
  502.0 1.4 fusion.37
  504.2 1.5 add_convert_fusion.1
  505.7 1.6 copy.69
  507.2 1.6 copy.68
  509.5 11.6 %all-reduce = bf16[3072]{0:T(1024)(128)(2,1)S(1)} all-reduce(bf16[3072]{0:T(1024)(128)(2,1)S(1)} %get-tuple-element.113), channel_id=9, replica_groups=mesh['rep'=8,'fsdp'=4] {'fsdp'}, use_global_device_ids=true, to_apply=%region_32.33.clone | all-reduce | flops 3072 | bytes 12288
  522.6 1.2 copy.78
  524.9 1.1 copy.82
  526.0 27.0 %reduce-scatter.16.cloned.1.call-done = bf16[192,768]{1,0:T(8,128)(2,1)} async-done(((bf16[768,768]{1,0:T(8,128)(2,1)}), bf16[192,768]{1,0:T(8,128)(2,1)}) %reduce-scatter.16.cloned.1.call-update) | async-done | bytes 294928 | tf_op jit(solution)/shard_map/reduce_scatter | solution.py:281
  553.0 86.1 %reduce-scatter.20.cloned.1.call-done = bf16[768,768]{1,0:T(8,128)(2,1)} async-done(((bf16[3072,768]{1,0:T(8,128)(2,1)}), bf16[768,768]{1,0:T(8,128)(2,1)}) %reduce-scatter.20.cloned.1.call-update) | async-done | bytes 1179664 | tf_op jit(solution)/shard_map/reduce_scatter | solution.py:287
  639.1 88.1 %reduce-scatter.18.cloned.1.call-done = bf16[192,3072]{1,0:T(8,128)(2,1)} async-done(((bf16[768,3072]{1,0:T(8,128)(2,1)}), bf16[192,3072]{1,0:T(8,128)(2,1)}) %reduce-scatter.18.cloned.1.call-update) | async-done | bytes 1179664 | tf_op jit(solution)/shard_map/reduce_scatter | solution.py:284
  727.2 155.7 %all-reduce.4 = (f32[192,768]{0,1:T(8,128)S(1)}, f32[192,768]{0,1:T(8,128)S(1)}, f32[192,768]{0,1:T(8,128)S(1)}, f32[192,768]{1,0:T(8,128)}, f32[192,3072]{1,0:T...) all-reduce(bf16[192,768]{0,1:T(8,128)(2,1)S(1)} %copy.78, ...), channel_id=1, replica_groups=mesh['rep'=8,'fsdp'=4] {'rep'}, use_global_device_ids=true, to_apply=%region_10.11 | all-reduce | flops 1771776 | bytes 10632192 | tf_op jit(solution)/shard_map/psum | solution.py:297
  (147 shorter events, 20.6 us)
Async XLA Ops:
  7.2 4.1 copy-start.23
  7.2 5.2 copy-start.26
  7.2 20.4 %copy-start.14 = (bf16[1024,768]{1,0:T(8,128)(2,1)S(1)}, bf16[1024,768]{1,0:T(8,128)(2,1)}, u32[]{:S(2)}) copy-start(bf16[1024,768]{1,0:T(8,128)(2,1)} %param.15) | copy-start | bytes 4718596
  7.2 39.6 %all-gather.11.cloned.1.call-start = ((), (), s32[]{:S(2)}) async-start(), calls=%async_computation.8 | async-start | bytes 1474560 | tf_op jit(solution)/shard_map/all_gather | solution.py:186
  7.9 66.0 %all-gather.13.cloned.1.call-start = ((), (), s32[]{:S(2)}) async-start(), calls=%async_computation.9 | async-start | bytes 1474560 | tf_op jit(solution)/shard_map/all_gather | solution.py:187
  8.7 96.4 %all-gather.9.cloned.1.call-start = ((), (), s32[]{:S(2)}) async-start(), calls=%async_computation.7 | async-start | bytes 1474560 | tf_op jit(solution)/shard_map/all_gather | solution.py:185
  9.4 129.4 %all-gather.15.cloned.1.call-start = ((), (), s32[]{:S(2)}) async-start(), calls=%async_computation.10 | async-start | bytes 1474560 | tf_op jit(solution)/shard_map/all_gather | solution.py:188
  10.0 216.1 %all-gather.17.cloned.1.call-start = ((), (), s32[]{:S(2)}) async-start(), calls=%async_computation.11 | async-start | bytes 5898240 | tf_op jit(solution)/shard_map/all_gather | solution.py:189
  10.6 19.1 %copy-start.28 = (s32[1,16,3]{1,0,2:T(1,128)S(1)}, s32[1,16,3]{1,0,2:T(1,128)}, u32[]{:S(2)}) copy-start(s32[1,16,3]{1,0,2:T(1,128)} %param.14) | copy-start | bytes 580
  10.6 19.3 %copy-start.17 = (bf16[1024,768]{1,0:T(8,128)(2,1)S(1)}, bf16[1024,768]{1,0:T(8,128)(2,1)}, u32[]{:S(2)}) copy-start(bf16[1024,768]{1,0:T(8,128)(2,1)} %param.12) | copy-start | bytes 4718596
  10.6 304.7 %all-gather.19.cloned.1.call-start = ((), (), s32[]{:S(2)}) async-start(), calls=%async_computation.12 | async-start | bytes 5898240 | tf_op jit(solution)/shard_map/all_gather | solution.py:190
  11.2 510.5 %reduce-scatter.28.cloned.1.call-start = ((), (), s32[]{:S(2)}) async-start(), calls=%async_computation.19 | async-start | bytes 245760
  29.3 2.3 copy-start.27
  29.6 17.0 %copy-start.22 = (bf16[1024,3]{1,0:T(8,128)(2,1)S(1)}, bf16[1024,3]{1,0:T(8,128)(2,1)}, u32[]{:S(2)}) copy-start(bf16[1024,3]{1,0:T(8,128)(2,1)} %fusion.18) | copy-start | bytes 18436
  49.5 58.3 %copy-start = (bf16[1024,768]{1,0:T(8,128)(2,1)}, bf16[1024,768]{1,0:T(8,128)(2,1)S(1)}, u32[]{:S(2)}) copy-start(bf16[1024,768]{1,0:T(8,128)(2,1)S(1)} %convolution_convert_fusion.3.k_ref) | copy-start | bytes 4718596
  105.1 2.7 copy-start.6
  137.7 1.1 copy-start.1
  138.8 5.7 copy-start.2
  144.5 1.6 copy-start.9
  315.4 13.4 %copy-start.13 = (bf16[1024,768]{0,1:T(8,128)(2,1)S(1)}, bf16[1024,768]{0,1:T(8,128)(2,1)}, u32[]{:S(2)}) copy-start(bf16[1024,768]{0,1:T(8,128)(2,1)} %copy.63) | copy-start | bytes 4718596
  333.6 17.6 %copy-start.19 = (bf16[1024,768]{0,1:T(8,128)(2,1)}, bf16[1024,768]{0,1:T(8,128)(2,1)S(1)}, u32[]{:S(2)}) copy-start(bf16[1024,768]{0,1:T(8,128)(2,1)S(1)} %get-tuple-element.94) | copy-start | bytes 4718596
  351.2 11.9 %copy-start.10 = (f32[1024,768]{0,1:T(8,128)S(1)}, f32[1024,768]{0,1:T(8,128)}, u32[]{:S(2)}) copy-start(f32[1024,768]{0,1:T(8,128)} %copy-done.9) | copy-start | bytes 9437188
  363.9 4.8 copy-start.11
  363.9 2.1 copy-start.21
  364.3 4.4 copy-start.16
  409.4 1.1 copy-start.7
  410.6 5.5 copy-start.4
  410.6 0.7 copy-start.25
  412.1 110.4 %reduce-scatter.22.cloned.1.call-start = ((), (), s32[]{:S(2)}) async-start(), calls=%async_computation.16 | async-start | bytes 1474560
  418.5 105.3 %reduce-scatter.24.cloned.1.call-start = ((), (), s32[]{:S(2)}) async-start(), calls=%async_computation.17 | async-start | bytes 1474560
  422.8 2.8 copy-start.18
  425.4 99.5 %reduce-scatter.26.cloned.1.call-start = ((), (), s32[]{:S(2)}) async-start(), calls=%async_computation.18 | async-start | bytes 1474560
  428.1 2.6 copy-start.3
  430.6 122.4 %reduce-scatter.16.cloned.1.call-start = ((), (), s32[]{:S(2)}) async-start(), calls=%async_computation.13 | async-start | bytes 1474560 | tf_op jit(solution)/shard_map/reduce_scatter | solution.py:281
  434.6 204.5 %reduce-scatter.20.cloned.1.call-start = ((), (), s32[]{:S(2)}) async-start(), calls=%async_computation.15 | async-start | bytes 5898240 | tf_op jit(solution)/shard_map/reduce_scatter | solution.py:287
  443.8 283.4 %reduce-scatter.18.cloned.1.call-start = ((), (), s32[]{:S(2)}) async-start(), calls=%async_computation.14 | async-start | bytes 5898240 | tf_op jit(solution)/shard_map/reduce_scatter | solution.py:284
  453.8 0.7 copy-start.30
  453.8 1.2 copy-start.24
  453.8 45.3 %copy-start.5 = (bf16[1024,768]{1,0:T(8,128)(2,1)S(1)}, bf16[1024,768]{1,0:T(8,128)(2,1)}, u32[]{:S(2)}) copy-start(bf16[1024,768]{1,0:T(8,128)(2,1)} %copy-done.4) | copy-start | bytes 4718596
  499.1 2.8 copy-start.8
  499.1 2.9 copy-start.29
  501.9 1.9 copy-start.12
  502.0 2.2 copy-start.20
  505.7 1.6 copy-start.15
Sparse Core Ops, SparseCore 0:
  9.6 33.2 all-gather.10
  44.5 29.4 all-gather.12
  75.5 29.4 all-gather.8
  106.5 29.4 all-gather.14
  137.4 88.6 all-gather.16
  227.5 87.7 all-gather.18
  412.3 17.9 reduce-scatter.27
  432.6 27.5 reduce-scatter.21
  462.5 28.8 reduce-scatter.23
  493.6 28.5 reduce-scatter.25
  525.1 27.8 reduce-scatter.15
  555.2 83.8 reduce-scatter.19
  641.4 85.7 reduce-scatter.17

commit v2 on v1

--- a/solution.py
+++ b/solution.py
@@ -109,6 +109,7 @@
         out_shape=[jax.ShapeDtypeStruct((SEQ_LEN,D),jnp.bfloat16),jax.ShapeDtypeStruct((H,SEQ_LEN,128),jnp.bfloat16)],
         scratch_shapes=[pltpu.VMEM((2,SEQ_LEN,256),jnp.bfloat16),pltpu.VMEM((SEQ_LEN,256),jnp.bfloat16),pltpu.VMEM((2,SEQ_LEN,128),jnp.bfloat16)],
         compiler_params=pltpu.CompilerParams(vmem_limit_bytes=48<<20),
+        cost_estimate=pl.CostEstimate(flops=30_000_000_000,bytes_accessed=10_000_000,transcendentals=12_582_912),
         name="attention_forward")(q,k,v,qf,kf)
 
 TK=256
@@ -164,7 +165,181 @@
         out_specs=[pair]*3,out_shape=[sd]*3,
         scratch_shapes=[pltpu.VMEM((2,SEQ_LEN,256),B),pltpu.VMEM((2,SEQ_LEN,256),B),pltpu.VMEM((SEQ_LEN,256),B),pltpu.VMEM((SEQ_LEN,256),B),pltpu.VMEM((2,SEQ_LEN,128),B),pltpu.VMEM((SEQ_LEN,128),jnp.float32)],
         compiler_params=pltpu.CompilerParams(vmem_limit_bytes=48<<20),
+        cost_estimate=pl.CostEstimate(flops=42_000_000_000,bytes_accessed=15_000_000,transcendentals=12_582_912),
         name="attention_backward")(q,k,v,do,o,aux,kf)
+
+
+def line_gather(piece):
+    count = lax.axis_size("fsdp")
+    place = lax.axis_index("fsdp")
+    held = [piece]
+    for step in range(1, count):
+        pairs = [(i, (i + step) % count) for i in range(count)]
+        held.append(lax.ppermute(piece, "fsdp", pairs))
+    turned = jnp.stack([held[(count - 1 - s) % count] for s in range(2 * count - 1)])
+    return lax.dynamic_slice_in_dim(turned, count - 1 - place, count, 0)
+
+
+def line_scatter(parts):
+    count = lax.axis_size("fsdp")
+    place = lax.axis_index("fsdp")
+    total = lax.dynamic_index_in_dim(parts, place, 0, False).astype(jnp.float32)
+    for step in range(1, count):
+        pairs = [(i, (i + step) % count) for i in range(count)]
+        sent = lax.dynamic_index_in_dim(parts, (place + step) % count, 0, False)
+        total = total + lax.ppermute(sent, "fsdp", pairs).astype(jnp.float32)
+    return total
+
+
+def rep_bit(bit):
+    return (lax.axis_index("rep") // (1 << bit)) % 2
+
+
+def swap(values, bit):
+    pairs = [(i, i ^ (1 << bit)) for i in range(lax.axis_size("rep"))]
+    return lax.ppermute(values, "rep", pairs)
+
+
+def ordered(bit, mine, other, join):
+    return jnp.where(rep_bit(bit) == 0, join(mine, other), join(other, mine))
+
+
+def join_at(axis):
+    return lambda a, b: jnp.stack([a, b], axis)
+
+
+def join_cols(a, b):
+    return jnp.concatenate([a, b], -1)
+
+
+def merge(values, bit, join):
+    return ordered(bit, values, swap(values, bit), join)
+
+
+def gather_square(shards):
+    kinds, rows, cols = shards.shape
+    rep = lax.axis_index("rep") % 8
+    half = cols // 2
+    piece = lax.dynamic_slice(
+        shards, (0, rep // 2 * (rows // 4), rep % 2 * half), (kinds, rows // 4, half)
+    )
+    lined = jnp.moveaxis(line_gather(piece), 0, 1)
+    left = merge(lined[..., : half // 2 // 128 * 128], 1, join_at(2))
+    left = merge(left, 2, join_at(2))
+    right = merge(lined[..., half // 2 // 128 * 128 :], 2, join_at(2))
+    right = merge(right, 1, join_at(3))
+    both = jnp.concatenate([left, right], -1)
+    both = merge(both, 0, join_cols)
+    return both.reshape(kinds, -1, cols)
+
+
+def gather_mlp(w_up, w_down):
+    rep = lax.axis_index("rep") % 8
+    cols = w_up.shape[1] // 8
+    rows = w_down.shape[0] // 8
+    up = line_gather(lax.dynamic_slice_in_dim(w_up, rep * cols, cols, 1))
+    up = up.reshape(-1, cols)
+    down = line_gather(
+        lax.dynamic_slice_in_dim(w_down, (rep % 2 * 4 + rep // 2) * rows, rows, 0)
+    )
+    up = merge(up, 1, join_cols)
+    down = merge(down, 2, join_at(1))
+    up = merge(up, 2, join_cols)
+    down = merge(down, 1, join_at(2)).reshape(-1, w_down.shape[1])
+    return up, swap(up, 0), down, swap(down, 0)
+
+
+def add_low(a, b):
+    return (a.astype(jnp.float32) + b.astype(jnp.float32)).astype(jnp.bfloat16)
+
+
+def fold(values, bit, take):
+    mine = rep_bit(bit)
+    return add_low(take(values, mine), swap(take(values, 1 - mine), bit))
+
+
+def take_at(axis):
+    return lambda values, i: lax.dynamic_index_in_dim(values, i, axis, False)
+
+
+def take_cols(values, i):
+    half = values.shape[-1] // 2
+    return lax.dynamic_slice_in_dim(values, i * half, half, values.ndim - 1)
+
+
+def take_inner(values, i):
+    part = values.shape[-1] // 4
+    return jnp.concatenate(
+        [lax.dynamic_slice_in_dim(values, (2 * j + i) * part, part, 1) for j in range(2)], 1
+    )
+
+
+def beyond(values):
+    bit = 3
+    while (1 << bit) < lax.axis_size("rep"):
+        values = add_low(values, swap(values, bit))
+        bit += 1
+    return values
+
+
+def reduce_square(grads):
+    kinds, rows, cols = grads.shape
+    count = lax.axis_size("fsdp")
+    part = fold(grads, 0, take_cols).reshape(kinds, count, 2, 2, -1, cols // 2)
+    cut = cols // 4 // 128 * 128
+    left = fold(part[..., :cut], 1, take_at(3))
+    left = fold(left, 2, take_at(2))
+    right = fold(part[..., cut:], 2, take_at(2))
+    right = fold(right, 1, take_at(2))
+    both = jnp.moveaxis(jnp.concatenate([left, right], -1), 1, 0)
+    both = beyond(line_scatter(both).astype(jnp.bfloat16))
+    left = merge(merge(both[..., :cut], 1, join_at(1)), 2, join_at(1))
+    right = merge(merge(both[..., cut:], 2, join_at(1)), 1, join_at(2))
+    both = merge(jnp.concatenate([left, right], -1), 0, join_cols)
+    return both.reshape(kinds, -1, cols).astype(jnp.float32)
+
+
+def reduce_up(grad):
+    count = lax.axis_size("fsdp")
+    part = fold(grad, 1, take_inner)
+    part = fold(part, 2, take_cols)
+    part = line_scatter(part.reshape(count, -1, part.shape[1]))
+    part = beyond(part.astype(jnp.bfloat16))
+    part = merge(part, 1, join_at(0))
+    part = merge(part, 2, join_at(0))
+    other = swap(part, 0)
+
+    def join(a, b):
+        return jnp.concatenate(
+            [v[y, x] for y in range(2) for x in range(2) for v in (a, b)], 1
+        ).astype(jnp.float32)
+
+    return ordered(0, part, other, join)
+
+
+def reduce_down(grad):
+    count = lax.axis_size("fsdp")
+    part = grad.reshape(count, 2, 2, -1, grad.shape[1])
+    part = fold(part, 2, take_at(1))
+    part = fold(part, 1, take_at(1))
+    part = beyond(line_scatter(part).astype(jnp.bfloat16))
+    part = merge(part, 1, join_at(0))
+    part = merge(part, 2, join_at(0))
+    part = merge(part, 0, join_at(0))
+    return part.reshape(-1, grad.shape[1]).astype(jnp.float32)
+
+
+def reduce_all(values):
+    bit = 0
+    while (1 << bit) < lax.axis_size("rep"):
+        values = values + swap(values, bit)
+        bit += 1
+    count = lax.axis_size("fsdp")
+    total = values
+    for step in range(1, count):
+        pairs = [(i, (i + step) % count) for i in range(count)]
+        total = total + lax.ppermute(values, "fsdp", pairs)
+    return total
 
 
 def per_device(
@@ -181,19 +356,19 @@
     vectors,
     up_bias,
 ):
-    gathered = (
-        lax.all_gather(w_query, "fsdp", axis=0, tiled=True),
-        lax.all_gather(w_key, "fsdp", axis=0, tiled=True),
-        lax.all_gather(w_value, "fsdp", axis=0, tiled=True),
-        lax.all_gather(w_out, "fsdp", axis=0, tiled=True),
-        lax.all_gather(w_up, "fsdp", axis=0, tiled=True),
-        lax.all_gather(w_down, "fsdp", axis=0, tiled=True),
-        lax.all_gather(vectors, "fsdp", axis=1, tiled=True),
-        lax.all_gather(up_bias, "fsdp", axis=0, tiled=True),
-    )
-    full_query, full_key, full_value, full_out, full_up, full_down, full_vectors, full_upbias = (
-        gathered
-    )
+    count = lax.axis_size("fsdp")
+    place = lax.axis_index("fsdp")
+    small = line_gather(jnp.concatenate([vectors, up_bias.reshape(4, -1)], 0))
+    full_vectors = jnp.moveaxis(small[:, :8], 0, 1).reshape(8, -1)
+    bias_halves = small[:, 8:].reshape(count, 2, -1).astype(jnp.float32)
+    core = rep_bit(0)
+    bias_mine = lax.dynamic_index_in_dim(bias_halves, core, 1, False).reshape(-1)
+    bias_other = lax.dynamic_index_in_dim(bias_halves, 1 - core, 1, False).reshape(-1)
+    first = gather_square(jnp.stack([w_query, w_key, w_value]))
+    full_query, full_key, full_value = first[0], first[1], first[2]
+    (full_out,) = gather_square(w_out[None])
+    up_mine, up_other, down_mine, down_other = gather_mlp(w_up, w_down)
+
     vec_float = full_vectors.astype(jnp.float32)
     inputs = tokens.astype(jnp.float32)
     q_low = (jnp.dot(tokens, full_query, preferred_element_type=jnp.float32) + vec_float[0]).astype(
@@ -209,12 +384,19 @@
     first_sum = inputs + attn_out
     normed_one, pull_one = jax.vjp(normalize, first_sum, vec_float[3], vec_float[4])
     normed_low = normed_one.astype(jnp.bfloat16)
-    up_proj = jnp.dot(normed_low, full_up, preferred_element_type=jnp.float32) + full_upbias.astype(
-        jnp.float32
-    )
-    activated, pull_gelu = jax.vjp(gelu_exact, up_proj)
-    activated_low = activated.astype(jnp.bfloat16)
-    mlp_out = jnp.dot(activated_low, full_down, preferred_element_type=jnp.float32) + vec_float[5]
+
+    def widen(weight, bias):
+        up_proj = jnp.dot(normed_low, weight, preferred_element_type=jnp.float32) + bias
+        activated, pull = jax.vjp(gelu_exact, up_proj)
+        return activated.astype(jnp.bfloat16), pull
+
+    act_mine, pull_mine = widen(up_mine, bias_mine)
+    act_other, pull_other = widen(up_other, bias_other)
+    mlp_out = (
+        jnp.dot(act_mine, down_mine, preferred_element_type=jnp.float32)
+        + jnp.dot(act_other, down_other, preferred_element_type=jnp.float32)
+        + vec_float[5]
+    )
     second_sum = normed_one + mlp_out
     layer_out, pull_two = jax.vjp(normalize, second_sum, vec_float[6], vec_float[7])
     valid = (segments >= 0).astype(jnp.float32)[:, None]
@@ -223,38 +405,39 @@
             jnp.sum(valid * first_sum * first_sum),
             jnp.sum(valid * attn_out * attn_out),
             jnp.sum(valid * mlp_out * mlp_out),
+            jnp.sum(valid),
         ]
     )
-    squares, counted = lax.psum((squares, jnp.sum(valid)), ("rep", "fsdp"))
-    rms_values = jnp.sqrt(squares / (counted * D))
-    regathered = (
-        lax.all_gather(w_query, "fsdp", axis=0, tiled=True),
-        lax.all_gather(w_key, "fsdp", axis=0, tiled=True),
-        lax.all_gather(w_value, "fsdp", axis=0, tiled=True),
-        lax.all_gather(w_out, "fsdp", axis=0, tiled=True),
-        lax.all_gather(w_up, "fsdp", axis=0, tiled=True),
-        lax.all_gather(w_down, "fsdp", axis=0, tiled=True),
-    )
-    back_query, back_key, back_value, back_out, back_up, back_down = regathered
     d_second, d_gain_two, d_shift_two = pull_two(out_grad.astype(jnp.float32))
     d_mlp = d_second.astype(jnp.bfloat16)
-    d_up = pull_gelu(dot_nt(d_mlp, back_down))[0].astype(jnp.bfloat16)
-    d_normed = d_second + dot_nt(d_up, back_up)
+
+    down_sent = swap(dot_tn(act_other, d_mlp).astype(jnp.bfloat16), 0)
+    d_up_other = pull_other(dot_nt(d_mlp, down_other))[0].astype(jnp.bfloat16)
+    up_sent = swap(dot_tn(normed_low, d_up_other).astype(jnp.bfloat16), 0)
+    d_up_mine = pull_mine(dot_nt(d_mlp, down_mine))[0].astype(jnp.bfloat16)
+    grad_down = reduce_down(
+        (dot_tn(act_mine, d_mlp) + down_sent.astype(jnp.float32)).astype(jnp.bfloat16)
+    )
+    grad_up = reduce_up(
+        (dot_tn(normed_low, d_up_mine) + up_sent.astype(jnp.float32)).astype(jnp.bfloat16)
+    )
+    d_normed = d_second + dot_nt(d_up_mine, up_mine) + dot_nt(d_up_other, up_other)
     d_first, d_gain_one, d_shift_one = pull_one(d_normed)
     d_attn = d_first.astype(jnp.bfloat16)
-    d_mixed = dot_nt(d_attn, back_out).astype(jnp.bfloat16)
+    d_mixed = dot_nt(d_attn, full_out).astype(jnp.bfloat16)
+    (grad_out,) = reduce_square(dot_tn(mixed_low, d_attn).astype(jnp.bfloat16)[None])
     dq_low, dk_low, dv_low = attention_backward(
         q_low, k_low, v_low, d_mixed, mixed_low, aux, k_feat
     )
+    grad_first = reduce_square(
+        jnp.stack([dot_tn(tokens, d).astype(jnp.bfloat16) for d in (dq_low, dk_low, dv_low)])
+    )
     tokens_grad = (
-        d_first + dot_nt(dq_low, back_query) + dot_nt(dk_low, back_key) + dot_nt(dv_low, back_value)
-    )
-    grad_query = dot_tn(tokens, dq_low)
-    grad_key = dot_tn(tokens, dk_low)
-    grad_value = dot_tn(tokens, dv_low)
-    grad_out = dot_tn(mixed_low, d_attn)
-    grad_up = dot_tn(normed_low, d_up)
-    grad_down = dot_tn(activated_low, d_mlp)
+        d_first + dot_nt(dq_low, full_query) + dot_nt(dk_low, full_key) + dot_nt(dv_low, full_value)
+    )
+    bias_mine = col_sums(d_up_mine).reshape(count, -1)
+    bias_other = col_sums(d_up_other).reshape(count, -1)
+    grad_bias = ordered(0, bias_mine, bias_other, join_cols)
     grad_vectors = jnp.stack(
         [
             col_sums(dq_low),
@@ -265,59 +448,24 @@
             col_sums(d_mlp),
             d_gain_two,
             d_shift_two,
+            jnp.zeros((D,), jnp.float32).at[:4].set(squares),
         ]
     )
-    grad_upbias = col_sums(d_up)
-    shard_sums = (
-        lax.psum_scatter(
-            grad_query.astype(jnp.bfloat16), "fsdp", scatter_dimension=0, tiled=True
-        ).astype(jnp.float32),
-        lax.psum_scatter(
-            grad_key.astype(jnp.bfloat16), "fsdp", scatter_dimension=0, tiled=True
-        ).astype(jnp.float32),
-        lax.psum_scatter(
-            grad_value.astype(jnp.bfloat16), "fsdp", scatter_dimension=0, tiled=True
-        ).astype(jnp.float32),
-        lax.psum_scatter(
-            grad_out.astype(jnp.bfloat16), "fsdp", scatter_dimension=0, tiled=True
-        ).astype(jnp.float32),
-        lax.psum_scatter(
-            grad_up.astype(jnp.bfloat16), "fsdp", scatter_dimension=0, tiled=True
-        ).astype(jnp.float32),
-        lax.psum_scatter(
-            grad_down.astype(jnp.bfloat16), "fsdp", scatter_dimension=0, tiled=True
-        ).astype(jnp.float32),
-        lax.psum_scatter(
-            grad_vectors.astype(jnp.bfloat16), "fsdp", scatter_dimension=1, tiled=True
-        ).astype(jnp.float32),
-        lax.psum_scatter(
-            grad_upbias.astype(jnp.bfloat16), "fsdp", scatter_dimension=0, tiled=True
-        ).astype(jnp.float32),
-    )
-    results = lax.psum(
-        (
-            shard_sums[0],
-            shard_sums[1],
-            shard_sums[2],
-            shard_sums[3],
-            shard_sums[4],
-            shard_sums[5],
-            shard_sums[6],
-            shard_sums[7],
-        ),
-        "rep",
-    )
+    sums = reduce_all(jnp.concatenate([grad_vectors, grad_bias.reshape(-1, D)], 0))
+    width = vectors.shape[1]
+    rms_values = jnp.sqrt(sums[8, :3] / (sums[8, 3] * D))
+    bias_sums = sums[9:].reshape(count, -1)
     return (
         layer_out.astype(jnp.bfloat16),
         tokens_grad.astype(jnp.bfloat16),
-        results[0],
-        results[1],
-        results[2],
-        results[3],
-        results[4],
-        results[5],
-        results[6],
-        results[7],
+        grad_first[0],
+        grad_first[1],
+        grad_first[2],
+        grad_out,
+        grad_up,
+        grad_down,
+        lax.dynamic_slice_in_dim(sums[:8], place * width, width, 1),
+        lax.dynamic_index_in_dim(bias_sums, place, 0, False),
         rms_values,
     )
 

time: 903 us -> 524 us (0.58)
  blocking collectives: 237 us -> 0 us
  waiting for transfers between devices: 388 us -> 161 us
  starting transfers between devices: 0.73 us -> 91.1 us
  other arithmetic: 12.9 us -> 31 us
  matrix products: 138 us -> 120 us
  between operations: 16.1 us -> 3.6 us
    reduce_scatter x3 -> x0, waiting for transfers between devices: 201 us -> none  [the longest x1 88.1 us: per_device(): lax.psum_scatter(grad_up.astype(jnp.bfloat16), 'fsdp', scatter_dimension=...]
    psum x2 -> x0, blocking collectives: 196 us -> none  [the longest x1 156 us: per_device(): lax.psum((shard_sums[0], shard_sums[1], shard_sums[2], shard_sums[3], sha...]
    all_gather x6 -> x0, waiting for transfers between devices: 183 us -> none  [the longest x1 79.5 us: per_device(): lax.all_gather(w_up, 'fsdp', axis=0, tiled=True)]
    ppermute x0 -> x81, waiting for transfers between devices: none -> 161 us  [the longest x51 128 us: swap(): return lax.ppermute(values, 'rep', pairs)]
    ppermute x0 -> x81, starting transfers between devices: none -> 91.1 us  [the longest x51 44.1 us: swap(): return lax.ppermute(values, 'rep', pairs)]
    all_gather x2 -> x0, blocking collectives: 28.5 us -> none  [the longest x1 15.1 us: per_device(): lax.all_gather(vectors, 'fsdp', axis=1, tiled=True)]
    unnamed x1 -> x0, blocking collectives: 11.6 us -> none
    dot_general x6 -> x8, matrix products: 33.6 us -> 22.8 us  [dot_tn(): lax.dot_general(left, right, (((0,), (0,)), ((), ())), preferred_element_...]
  transfers between devices with their start and end apart: 13 -> 81, of which waited for: 7 -> 40; matrix products, arithmetic and copies ran while one was open for 13% -> 22% of each run, Pallas kernels for 3% -> 6%
where the time goes in v2:
time: 524 us; the launch traced here: 516 us
  waiting for transfers between devices  161 us (31%)
  matrix products  120 us (23%)
  starting transfers between devices  91.1 us (17%)
  Pallas kernels  71.6 us (14%)
  local copies, waits for them, and re-layouts  37.6 us (7%)
  other arithmetic  31 us (6%)
    ppermute x51, waiting for transfers between devices, swap(): return lax.ppermute(values, 'rep', pairs)  128 us
    ppermute x51, starting transfers between devices, swap(): return lax.ppermute(values, 'rep', pairs)  44.1 us
    pallas_call x1, Pallas kernels, attention_backward(): pl.pallas_call(bwd_kernel, grid=(H // 2,), in_specs=[pair] * 5 + [pl.Bloc...  41.1 us
    dot_general x2, matrix products, widen(): jnp.dot(normed_low, weight, preferred_element_type=jnp.float32) + bias  38.6 us
    dot_general x8, matrix products, dot_nt(): lax.dot_general(left, right, (((1,), (1,)), ((), ())), preferred_element_...  37.6 us
    pallas_call x1, Pallas kernels, attention_forward(): pl.pallas_call(fwd_kernel, grid=(H // 2,), in_specs=[pair, pair, pair, wh...  30.5 us
    ppermute x15, starting transfers between devices, line_gather(): held.append(lax.ppermute(piece, 'fsdp', pairs))  23.2 us
    dot_general x8, matrix products, dot_tn(): lax.dot_general(left, right, (((0,), (0,)), ((), ())), preferred_element_...  22.8 us
  transfers between devices with their start and end apart: 81, of which 40 were waited for; matrix products, arithmetic and copies ran while one was open for 22% of the time, Pallas kernels for 6%

profile of v2, /device:TPU:0, one launch (start us, length us, event | category | flops | bytes accessed | tf_op | source)
XLA Modules:
  0.0 515.7 jit_solution(13026582118999669077)
XLA Ops:
  2.3 5.1 collective-permute-start.24
  11.0 2.8 collective-permute-start.8
  29.2 3.8 collective-permute-start.11
  51.0 4.6 collective-permute-done.1
  55.6 2.6 collective-permute-start.19
  60.2 3.8 collective-permute-done.16
  64.0 2.7 collective-permute-start.20
  77.1 3.0 collective-permute-done.5
  81.8 9.0 %collective-permute-done.4 = bf16[3,4,2,48,128]{4,3,2,1,0:T(8,128)(2,1)S(1)} collective-permute-done((bf16[3,4,2,48,128]{4,3,2,1,0:T(8,128)(2,1)S(1)}, bf16[3,4,2,48,128]{4,3,2,1,0:T(8,128)(2,1)S(1)}, u32[]{:S(2)}, u32[]{:S(2)}) %collective-permute-start.4) | collective-permute-done | bytes 294944 | tf_op jit(solution)/shard_map/ppermute | solution.py:200
  95.8 11.9 %collective-permute-done.22 = bf16[768,384]{1,0:T(8,128)(2,1)S(1)} collective-permute-done((bf16[768,384]{1,0:T(8,128)(2,1)S(1)}, bf16[768,384]{1,0:T(8,128)(2,1)S(1)}, u32[]{:S(2)}, u32[]{:S(2)}) %collective-permute-start.22) | collective-permute-done | bytes 589856 | tf_op jit(solution)/shard_map/ppermute | solution.py:200
  111.6 16.5 %collective-permute-done.28 = bf16[4,2,96,768]{3,2,1,0:T(8,128)(2,1)S(1)} collective-permute-done((bf16[4,2,96,768]{3,2,1,0:T(8,128)(2,1)S(1)}, bf16[4,2,96,768]{3,2,1,0:T(8,128)(2,1)S(1)}, u32[]{:S(2)}, u32[]{:S(2)}) %collective-permute-start.28) | collective-permute-done | bytes 1179680 | tf_op jit(solution)/shard_map/ppermute | solution.py:200
  138.0 30.5 %attention_forward.1 = (bf16[1024,768]{1,0:T(8,128)(2,1)S(1)}, bf16[12,1024,128]{2,1,0:T(8,128)(2,1)}) custom-call(bf16[1024,768]{1,0:T(8,128)(2,1)S(1)} %fusion.23.q_ref, bf16[1024,768]{1,0:T(8,128)(2,1)S(1)} %fusion.22.k_ref, bf16[1024,768]{1,0:T(8,128)(2,1)} %fusion.24.v_ref, bf16[1024,128]{1,0:T(8,128)(2,1)S(1)} %get-tuple-element.185.qf_ref, ...), custom_call_target="tpu_custom_call" | custom-call | flops 30000001024 | bytes 10000000 | tf_op jit(solution)/shard_map/attention_forward/pallas_call | solution.py:106
  171.1 18.8 %multiply_convert_fusion.1 = (bf16[1024,1536]{1,0:T(8,128)(2,1)S(1)}, f32[1024,1536]{1,0:T(8,128)}, f32[1024,1536]{1,0:T(8,128)}) fusion(f32[1536]{0:T(1024)S(1)} %add.501, bf16[1024,768]{0,1:T(8,128)(2,1)S(1)} %fusion.20, bf16[768,1536]{1,0:T(8,128)(2,1)S(1)} %maximum_select_fusion.1), kind=kOutput, calls=%fused_computation.21 | convolution fusion | flops 2519728128 | bytes 19666944 | tf_op jit(solution)/shard_map/dot_general | solution.py:389
  190.0 19.8 %multiply_convert_fusion = (bf16[1024,1536]{1,0:T(8,128)(2,1)S(1)}, f32[1024,1536]{1,0:T(8,128)}, f32[1024,1536]{1,0:T(8,128)}) fusion(f32[1536]{0:T(1024)S(1)} %add.507, bf16[1024,768]{0,1:T(8,128)(2,1)S(1)} %fusion.20, bf16[768,1536]{1,0:T(8,128)(2,1)} %collective-permute-done.29), kind=kOutput, calls=%fused_computation.8 | convolution fusion | flops 2519728128 | bytes 19666944 | tf_op jit(solution)/shard_map/dot_general | solution.py:389
  209.7 7.2 %fusion.111 = f32[1024,768]{0,1:T(8,128)} fusion(bf16[1024,1536]{1,0:T(8,128)(2,1)S(1)} %get-tuple-element.100, bf16[1536,768]{1,0:T(8,128)(2,1)} %collective-permute-done.30), kind=kOutput, calls=%fused_computation.406 | convolution fusion | flops 2415919104 | bytes 8650752 | tf_op jit(solution)/shard_map/dot_general | solution.py:397
  216.9 6.6 %fusion.17 = (f32[]{:T(128)}, f32[]{:T(128)}, f32[1024]{0:T(1024)S(1)}, f32[1024,768]{0,1:T(8,128)S(1)}) fusion(f32[1024,768]{0,1:T(8,128)S(1)} %get-tuple-element.182, f32[1024]{0:T(1024)S(1)} %copy-done.36, f32[768]{0:T(1024)S(1)} %add.491, f32[768]{0:T(1024)S(1)} %copy-done.38, f32[1024,768]{0,1:T(8,128)} %fusion.111, f32[768]{0:T(1024)S(1)} %add.496, ...), kind=kOutput, calls=%fused_computation.56 | convolution fusion | flops 2427714560 | bytes 18116616 | tf_op jit(solution)/shard_map/dot_general | solution.py:396
  228.1 3.9 convolution_convert_fusion
  232.0 7.5 %convert_reduce_fusion.1 = (f32[1536]{0:T(1024)S(1)}, bf16[1024,1536]{1,0:T(8,128)(2,1)S(1)}) fusion(f32[1024,1536]{1,0:T(8,128)} %get-tuple-element.103, f32[1024,1536]{1,0:T(8,128)} %get-tuple-element.183, f32[1536]{0:T(1024)S(1)} %add.501, bf16[1024,768]{0,1:T(8,128)(2,1)S(1)} %get-tuple-element.92, bf16[1536,768]{1,0:T(8,128)(2,1)S(1)} %bitcast.447), kind=kOutput, calls=%fused_computation.5 | convolution fusion | flops 2442656256 | bytes 19673088 | tf_op jit(solution)/shard_map/dot_general | solution.py:37
  239.6 2.6 fusion.112
  242.2 8.5 %convert_reduce_fusion = (f32[1536]{0:T(1024)S(1)}, bf16[1024,1536]{1,0:T(8,128)(2,1)S(1)}) fusion(f32[1024,1536]{1,0:T(8,128)} %get-tuple-element.101, f32[1024,1536]{1,0:T(8,128)} %get-tuple-element.184, f32[1536]{0:T(1024)S(1)} %add.507, bf16[1024,768]{0,1:T(8,128)(2,1)S(1)} %get-tuple-element.92, bf16[1536,768]{1,0:T(8,128)(2,1)} %collective-permute-done.30), kind=kOutput, calls=%fused_computation.4 | convolution fusion | flops 2442656256 | bytes 19673088 | tf_op jit(solution)/shard_map/dot_general | solution.py:37
  250.7 4.0 convolution_convert_fusion.1
  254.7 7.7 %multiply_reduce_fusion = (f32[768]{0:T(1024)S(1)}, f32[1024]{0:T(1024)S(1)}, f32[]{:T(128)}, f32[768]{0:T(1024)S(1)}, f32[1024,768]{0,1:T(8,128)S(1)}, /*index=5*/bf16[1024,768]{0,1:T(8,128)(2,1)}) fusion(f32[1024,768]{0,1:T(8,128)S(1)} %get-tuple-element.105, f32[1024]{0:T(1024)S(1)} %fusion.96, f32[1024]{0:T(1024)S(1)} %broadcast_multiply_fusion.1, ...), kind=kOutput, calls=%fused_computation.59 | convolution fusion | flops 2435577344 | bytes 21281796 | tf_op jit(solution)/shard_map/dot_general | solution.py:37
  265.4 2.6 convolution_convert_fusion.3.do_ref
  270.5 41.1 %attention_backward.1 = (bf16[1024,768]{1,0:T(8,128)(2,1)S(1)}, bf16[1024,768]{1,0:T(8,128)(2,1)S(1)}, bf16[1024,768]{1,0:T(8,128)(2,1)S(1)}) custom-call(bf16[1024,768]{1,0:T(8,128)(2,1)} %copy-done.5, bf16[1024,768]{1,0:T(8,128)(2,1)} %copy-done.4, bf16[1024,768]{1,0:T(8,128)(2,1)} %fusion.24.v_ref, bf16[1024,768]{1,0:T(8,128)(2,1)} %convolution_convert_fusion.3.do_ref, ...), custom_call_target="tpu_custom_call" | custom-call | flops 41999998976 | bytes 15000000 | tf_op jit(solution)/shard_map/attention_backward/pallas_call | solution.py:163
  314.4 3.1 fusion.113
  317.9 2.7 maximum_bitcast_fusion.3
  323.1 2.8 fusion.114
  326.7 2.6 add_convert_fusion.5
  340.0 3.6 collective-permute-start.80
  345.0 2.6 copy.148
  356.6 3.0 collective-permute-done.45
  364.1 4.2 collective-permute-done.48
  370.5 3.0 collective-permute-start.51
  384.1 6.3 %collective-permute-done.32 = bf16[3,4,2,48,128]{4,3,1,0,2:T(8,128)(2,1)S(1)} collective-permute-done((bf16[3,4,2,48,128]{4,3,1,0,2:T(8,128)(2,1)S(1)}, bf16[3,4,2,48,128]{4,3,1,0,2:T(8,128)(2,1)S(1)}, u32[]{:S(2)}, u32[]{:S(2)}) %collective-permute-start.32) | collective-permute-done | bytes 294944 | tf_op jit(solution)/shard_map/ppermute | solution.py:200
  393.0 4.4 collective-permute-done.33
  397.4 4.2 add_convert_fusion.2
  402.9 7.1 %collective-permute-done.34 = bf16[3,4,2,48,256]{4,3,2,1,0:T(8,128)(2,1)S(1)} collective-permute-done((bf16[3,4,2,48,256]{4,3,2,1,0:T(8,128)(2,1)S(1)}, bf16[3,4,2,48,256]{4,3,2,1,0:T(8,128)(2,1)S(1)}, u32[]{:S(2)}, u32[]{:S(2)}) %collective-permute-start.34) | collective-permute-done | bytes 589856 | tf_op jit(solution)/shard_map/ppermute | solution.py:200
  411.4 2.8 add_convert_fusion.3
  414.5 3.7 collective-permute-done.35
  418.4 3.1 collective-permute-start.36
  421.5 3.5 collective-permute-start.37
  432.9 11.7 %collective-permute-done.39 = bf16[3,48,128]{2,1,0:T(8,128)(2,1)S(1)} collective-permute-done((bf16[3,48,128]{2,1,0:T(8,128)(2,1)S(1)}, bf16[3,48,128]{2,1,0:T(8,128)(2,1)S(1)}, u32[]{:S(2)}, u32[]{:S(2)}) %collective-permute-start.39) | collective-permute-done | bytes 36896 | tf_op jit(solution)/shard_map/ppermute | solution.py:200
  455.5 12.0 %collective-permute-done.68 = bf16[4,96,768]{2,1,0:T(8,128)(2,1)S(1)} collective-permute-done((bf16[4,96,768]{2,1,0:T(8,128)(2,1)S(1)}, bf16[4,96,768]{2,1,0:T(8,128)(2,1)S(1)}, u32[]{:S(2)}, u32[]{:S(2)}) %collective-permute-start.68) | collective-permute-done | bytes 589856 | tf_op jit(solution)/shard_map/ppermute | solution.py:200
  468.6 2.8 collective-permute-start.70
  478.5 7.9 %collective-permute-done.70 = bf16[96,768]{1,0:T(8,128)(2,1)S(1)} collective-permute-done((bf16[96,768]{1,0:T(8,128)(2,1)S(1)}, bf16[96,768]{1,0:T(8,128)(2,1)S(1)}, u32[]{:S(2)}, u32[]{:S(2)}) %collective-permute-start.70) | collective-permute-done | bytes 147488 | tf_op jit(solution)/shard_map/ppermute | solution.py:190
  487.4 6.5 %collective-permute-done.61 = bf16[192,384]{1,0:T(8,128)(2,1)S(1)} collective-permute-done((bf16[192,384]{1,0:T(8,128)(2,1)S(1)}, bf16[192,384]{1,0:T(8,128)(2,1)S(1)}, u32[]{:S(2)}, u32[]{:S(2)}) %collective-permute-start.61) | collective-permute-done | bytes 147488 | tf_op jit(solution)/shard_map/ppermute | solution.py:190
  500.9 5.3 %collective-permute-done.73 = bf16[2,96,768]{2,1,0:T(8,128)(2,1)S(1)} collective-permute-done((bf16[2,96,768]{2,1,0:T(8,128)(2,1)S(1)}, bf16[2,96,768]{2,1,0:T(8,128)(2,1)S(1)}, u32[]{:S(2)}, u32[]{:S(2)}) %collective-permute-start.73) | collective-permute-done | bytes 294944 | tf_op jit(solution)/shard_map/ppermute | solution.py:200
  506.4 4.8 collective-permute-done.64
  (484 shorter events, 171.9 us)
Async XLA Ops:
  2.3 64.5 %collective-permute-start.24 = (bf16[96,768]{1,0:T(8,128)(2,1)}, bf16[96,768]{1,0:T(8,128)(2,1)S(1)}, u32[]{:S(2)}, u32[]{:S(2)}) collective-permute-start(bf16[96,768]{1,0:T(8,128)(2,1)} %constant_dynamic-slice_fusion.15), channel_id=1, source_target_pairs={{0,3},{1,0},{2,1},{3,2},{4,7},{5,4},{6,5},{7,6},{8,11},{9,8},{10,9... | collective-permute-start | bytes 442376 | tf_op jit(solution)/shard_map/ppermute | solution.py:178
  7.4 59.5 %collective-permute-start.25 = (bf16[96,768]{1,0:T(8,128)(2,1)}, bf16[96,768]{1,0:T(8,128)(2,1)S(1)}, u32[]{:S(2)}, u32[]{:S(2)}) collective-permute-start(bf16[96,768]{1,0:T(8,128)(2,1)} %constant_dynamic-slice_fusion.15), channel_id=1, source_target_pairs={{0,2},{1,3},{2,0},{3,1},{4,6},{5,7},{6,4},{7,5},{8,10},{9,11},{10,... | collective-permute-start | bytes 442376 | tf_op jit(solution)/shard_map/ppermute | solution.py:178
  7.4 61.1 %collective-permute-start.26 = (bf16[96,768]{1,0:T(8,128)(2,1)}, bf16[96,768]{1,0:T(8,128)(2,1)S(1)}, u32[]{:S(2)}, u32[]{:S(2)}) collective-permute-start(bf16[96,768]{1,0:T(8,128)(2,1)} %constant_dynamic-slice_fusion.15), channel_id=1, source_target_pairs={{0,1},{1,2},{2,3},{3,0},{4,5},{5,6},{6,7},{7,4},{8,9},{9,10},{10,1... | collective-permute-start | bytes 442376 | tf_op jit(solution)/shard_map/ppermute | solution.py:178
  11.0 18.2 %collective-permute-start.8 = (bf16[12,192]{1,0:T(8,128)(2,1)}, bf16[12,192]{1,0:T(8,128)(2,1)S(1)}, u32[]{:S(2)}, u32[]{:S(2)}) collective-permute-start(bf16[12,192]{1,0:T(8,128)(2,1)} %constant_dynamic-update-slice_fusion.7), channel_id=1, source_target_pairs={{0,3},{1,0},{2,1},{3,2},{4,7},{5,4},{6,5},{7,6},{8,11},{9,8},{10,9... | collective-permute-start | bytes 13832 | tf_op jit(solution)/shard_map/ppermute | solution.py:178
  13.8 15.4 %collective-permute-start.9 = (bf16[12,192]{1,0:T(8,128)(2,1)}, bf16[12,192]{1,0:T(8,128)(2,1)S(1)}, u32[]{:S(2)}, u32[]{:S(2)}) collective-permute-start(bf16[12,192]{1,0:T(8,128)(2,1)} %constant_dynamic-update-slice_fusion.7), channel_id=1, source_target_pairs={{0,2},{1,3},{2,0},{3,1},{4,6},{5,7},{6,4},{7,5},{8,10},{9,11},{10,... | collective-permute-start | bytes 13832 | tf_op jit(solution)/shard_map/ppermute | solution.py:178
  29.2 9.1 %collective-permute-start.11 = (bf16[1,48,384]{2,1,0:T(8,128)(2,1)}, bf16[1,48,384]{2,1,0:T(8,128)(2,1)S(1)}, u32[]{:S(2)}, u32[]{:S(2)}) collective-permute-start(bf16[1,48,384]{2,1,0:T(8,128)(2,1)} %dynamic-slice_bitcast_fusion.17), channel_id=1, source_target_pairs={{0,3},{1,0},{2,1},{3,2},{4,7},{5,4},{6,5},{7,6},{8,11},{9,8},{10,9... | collective-permute-start | bytes 110600 | tf_op jit(solution)/shard_map/ppermute | solution.py:178
  40.0 10.5 %collective-permute-start = (bf16[3,48,384]{2,1,0:T(8,128)(2,1)S(1)}, bf16[3,48,384]{2,1,0:T(8,128)(2,1)S(1)}, u32[]{:S(2)}, u32[]{:S(2)}) collective-permute-start(bf16[3,48,384]{2,1,0:T(8,128)(2,1)S(1)} %fusion.67), channel_id=1, source_target_pairs={{0,3},{1,0},{2,1},{3,2},{4,7},{5,4},{6,5},{7,6},{8,11},{9,8},{10,9... | collective-permute-start | bytes 331784 | tf_op jit(solution)/shard_map/ppermute | solution.py:178
  55.6 14.5 %collective-permute-start.19 = (bf16[192,384]{1,0:T(8,128)(2,1)}, bf16[192,384]{1,0:T(8,128)(2,1)S(1)}, u32[]{:S(2)}, u32[]{:S(2)}) collective-permute-start(bf16[192,384]{1,0:T(8,128)(2,1)} %constant_dynamic-slice_fusion.18), channel_id=1, source_target_pairs={{0,3},{1,0},{2,1},{3,2},{4,7},{5,4},{6,5},{7,6},{8,11},{9,8},{10,9... | collective-permute-start | bytes 442376 | tf_op jit(solution)/shard_map/ppermute | solution.py:178
  66.9 42.3 %collective-permute-start.15 = (bf16[1,4,2,48,128]{4,3,2,1,0:T(8,128)(2,1)S(1)}, bf16[1,4,2,48,128]{4,3,2,1,0:T(8,128)(2,1)S(1)}, u32[]{:S(2)}, u32[]{:S(2)}) collective-permute-start(bf16[1,4,2,48,128]{4,3,2,1,0:T(8,128)(2,1)S(1)} %maximum_select_fusion.30), channel_id=1, source_target_pairs={{0,16},{4,20},{8,24},{12,28},{16,0},{20,4},{24,8},{28,12},{1,17},{... | collective-permute-start | bytes 294920 | tf_op jit(solution)/shard_map/ppermute | solution.py:200
  68.5 8.0 %collective-permute-start.3 = (bf16[3,4,48,128]{3,2,1,0:T(8,128)(2,1)S(1)}, bf16[3,4,48,128]{3,2,1,0:T(8,128)(2,1)S(1)}, u32[]{:S(2)}, u32[]{:S(2)}) collective-permute-start(bf16[3,4,48,128]{3,2,1,0:T(8,128)(2,1)S(1)} %get-tuple-element.150), channel_id=1, source_target_pairs={{0,8},{4,12},{8,0},{12,4},{16,24},{20,28},{24,16},{28,20},{1,9},{5... | collective-permute-start | bytes 442376 | tf_op jit(solution)/shard_map/ppermute | solution.py:200
  70.1 9.9 %collective-permute-start.5 = (bf16[3,4,48,256]{3,2,1,0:T(8,128)(2,1)S(1)}, bf16[3,4,48,256]{3,2,1,0:T(8,128)(2,1)S(1)}, u32[]{:S(2)}, u32[]{:S(2)}) collective-permute-start(bf16[3,4,48,256]{3,2,1,0:T(8,128)(2,1)S(1)} %get-tuple-element.153), channel_id=1, source_target_pairs={{0,16},{4,20},{8,24},{12,28},{16,0},{20,4},{24,8},{28,12},{1,17},{... | collective-permute-start | bytes 884744 | tf_op jit(solution)/shard_map/ppermute | solution.py:200
  71.7 37.6 %collective-permute-start.17 = (bf16[1,4,2,48,256]{4,3,1,2,0:T(8,128)(2,1)S(1)}, bf16[1,4,2,48,256]{4,3,1,2,0:T(8,128)(2,1)S(1)}, u32[]{:S(2)}, u32[]{:S(2)}) collective-permute-start(bf16[1,4,2,48,256]{4,3,1,2,0:T(8,128)(2,1)S(1)} %maximum_select_fusion.25), channel_id=1, source_target_pairs={{0,8},{4,12},{8,0},{12,4},{16,24},{20,28},{24,16},{28,20},{1,9},{5... | collective-permute-start | bytes 589832 | tf_op jit(solution)/shard_map/ppermute | solution.py:200
  73.8 17.7 %collective-permute-start.27 = (bf16[4,96,768]{2,1,0:T(8,128)(2,1)S(1)}, bf16[4,96,768]{2,1,0:T(8,128)(2,1)S(1)}, u32[]{:S(2)}, u32[]{:S(2)}) collective-permute-start(bf16[4,96,768]{2,1,0:T(8,128)(2,1)S(1)} %constant_dynamic-slice_fusion.14), channel_id=1, source_target_pairs={{0,16},{4,20},{8,24},{12,28},{16,0},{20,4},{24,8},{28,12},{1,17},{... | collective-permute-start | bytes 1769480 | tf_op jit(solution)/shard_map/ppermute | solution.py:200
  76.5 14.3 %collective-permute-start.4 = (bf16[3,4,2,48,128]{4,3,2,1,0:T(8,128)(2,1)S(1)}, bf16[3,4,2,48,128]{4,3,2,1,0:T(8,128)(2,1)S(1)}, u32[]{:S(2)}, u32[]{:S(2)}) collective-permute-start(bf16[3,4,2,48,128]{4,3,2,1,0:T(8,128)(2,1)S(1)} %maximum_select_fusion.16), channel_id=1, source_target_pairs={{0,16},{4,20},{8,24},{12,28},{16,0},{20,4},{24,8},{28,12},{1,17},{... | collective-permute-start | bytes 884744 | tf_op jit(solution)/shard_map/ppermute | solution.py:200
  80.2 14.9 %collective-permute-start.6 = (bf16[3,4,2,48,256]{4,3,1,0,2:T(8,128)(2,1)S(1)}, bf16[3,4,2,48,256]{4,3,1,0,2:T(8,128)(2,1)S(1)}, u32[]{:S(2)}, u32[]{:S(2)}) collective-permute-start(bf16[3,4,2,48,256]{4,3,1,0,2:T(8,128)(2,1)S(1)} %maximum_select_fusion.10), channel_id=1, source_target_pairs={{0,8},{4,12},{8,0},{12,4},{16,24},{20,28},{24,16},{28,20},{1,9},{5... | collective-permute-start | bytes 1769480 | tf_op jit(solution)/shard_map/ppermute | solution.py:200
  90.8 16.9 %collective-permute-start.22 = (bf16[768,384]{1,0:T(8,128)(2,1)S(1)}, bf16[768,384]{1,0:T(8,128)(2,1)S(1)}, u32[]{:S(2)}, u32[]{:S(2)}) collective-permute-start(bf16[768,384]{1,0:T(8,128)(2,1)S(1)} %bitcast.441), channel_id=1, source_target_pairs={{0,8},{4,12},{8,0},{12,4},{16,24},{20,28},{24,16},{28,20},{1,9},{5... | collective-permute-start | bytes 1769480 | tf_op jit(solution)/shard_map/ppermute | solution.py:200
  91.6 36.5 %collective-permute-start.28 = (bf16[4,2,96,768]{3,2,1,0:T(8,128)(2,1)S(1)}, bf16[4,2,96,768]{3,2,1,0:T(8,128)(2,1)S(1)}, u32[]{:S(2)}, u32[]{:S(2)}) collective-permute-start(bf16[4,2,96,768]{3,2,1,0:T(8,128)(2,1)S(1)} %maximum_select_fusion.5), channel_id=1, source_target_pairs={{0,8},{4,12},{8,0},{12,4},{16,24},{20,28},{24,16},{28,20},{1,9},{5... | collective-permute-start | bytes 3538952 | tf_op jit(solution)/shard_map/ppermute | solution.py:200
  95.7 34.3 %collective-permute-start.7 = (bf16[3,4,2,2,48,384]{5,4,3,2,1,0:T(8,128)(2,1)S(1)}, bf16[3,4,2,2,48,384]{5,4,3,2,1,0:T(8,128)(2,1)S(1)}, u32[]{:S(2)}, u32[]{:S(2)}) collective-permute-start(bf16[3,4,2,2,48,384]{5,4,3,2,1,0:T(8,128)(2,1)S(1)} %pad_maximum_fusion.1), channel_id=1, source_target_pairs={{0,4},{4,0},{8,12},{12,8},{16,20},{20,16},{24,28},{28,24},{1,5},{5... | collective-permute-start | bytes 5308424 | tf_op jit(solution)/shard_map/ppermute | solution.py:200
  108.0 20.4 %collective-permute-start.23 = (bf16[768,768]{1,0:T(8,128)(2,1)S(1)}, bf16[768,768]{1,0:T(8,128)(2,1)S(1)}, u32[]{:S(2)}, u32[]{:S(2)}) collective-permute-start(bf16[768,768]{1,0:T(8,128)(2,1)S(1)} %maximum_select_fusion.4), channel_id=1, source_target_pairs={{0,16},{4,20},{8,24},{12,28},{16,0},{20,4},{24,8},{28,12},{1,17},{... | collective-permute-start | bytes 3538952 | tf_op jit(solution)/shard_map/ppermute | solution.py:200
  128.3 81.5 %collective-permute-start.30 = (bf16[1536,768]{1,0:T(8,128)(2,1)S(1)}, bf16[1536,768]{1,0:T(8,128)(2,1)}, u32[]{:S(2)}, u32[]{:S(2)}) collective-permute-start(bf16[1536,768]{1,0:T(8,128)(2,1)S(1)} %bitcast.445), channel_id=1, source_target_pairs={{0,4},{4,0},{8,12},{12,8},{16,20},{20,16},{24,28},{28,24},{1,5},{5... | collective-permute-start | bytes 7077896 | tf_op jit(solution)/shard_map/ppermute | solution.py:200
  129.4 60.5 %collective-permute-start.29 = (bf16[768,1536]{1,0:T(8,128)(2,1)S(1)}, bf16[768,1536]{1,0:T(8,128)(2,1)}, u32[]{:S(2)}, u32[]{:S(2)}) collective-permute-start(bf16[768,1536]{1,0:T(8,128)(2,1)S(1)} %maximum_select_fusion.1), channel_id=1, source_target_pairs={{0,4},{4,0},{8,12},{12,8},{16,20},{20,16},{24,28},{28,24},{1,5},{5... | collective-permute-start | bytes 7077896 | tf_op jit(solution)/shard_map/ppermute | solution.py:200
  320.6 10.2 %collective-permute-start.75 = (f32[13,768]{1,0:T(8,128)S(1)}, f32[13,768]{1,0:T(8,128)S(1)}, u32[]{:S(2)}, u32[]{:S(2)}) collective-permute-start(f32[13,768]{1,0:T(8,128)S(1)} %concatenate.556), channel_id=1, source_target_pairs={{0,4},{4,0},{8,12},{12,8},{16,20},{20,16},{24,28},{28,24},{1,5},{5... | collective-permute-start | bytes 119816 | tf_op jit(solution)/shard_map/ppermute | solution.py:200
  322.7 30.3 %collective-permute-start.44 = (bf16[1,768,384]{2,1,0:T(8,128)(2,1)}, bf16[1,768,384]{2,1,0:T(8,128)(2,1)}, u32[]{:S(2)}, u32[]{:S(2)}) collective-permute-start(bf16[1,768,384]{2,1,0:T(8,128)(2,1)} %dynamic-slice_bitcast_fusion.2), channel_id=1, source_target_pairs={{0,4},{4,0},{8,12},{12,8},{16,20},{20,16},{24,28},{28,24},{1,5},{5... | collective-permute-start | bytes 1769480 | tf_op jit(solution)/shard_map/ppermute | solution.py:200
  333.8 63.6 %collective-permute-start.66 = (bf16[1536,768]{1,0:T(8,128)(2,1)}, bf16[1536,768]{1,0:T(8,128)(2,1)}, u32[]{:S(2)}, u32[]{:S(2)}) collective-permute-start(bf16[1536,768]{1,0:T(8,128)(2,1)} %convolution_convert_fusion), channel_id=1, source_target_pairs={{0,4},{4,0},{8,12},{12,8},{16,20},{20,16},{24,28},{28,24},{1,5},{5... | collective-permute-start | bytes 7077896 | tf_op jit(solution)/shard_map/ppermute | solution.py:200
  339.8 10.4 %collective-permute-start.78 = (f32[13,768]{1,0:T(8,128)}, f32[13,768]{1,0:T(8,128)}, u32[]{:S(2)}, u32[]{:S(2)}) collective-permute-start(f32[13,768]{1,0:T(8,128)} %add.576), channel_id=1, source_target_pairs={{0,1},{1,2},{2,3},{3,0},{4,5},{5,6},{6,7},{7,4},{8,9},{9,10},{10,1... | collective-permute-start | bytes 119816 | tf_op jit(solution)/shard_map/ppermute | solution.py:341
  339.8 10.4 %collective-permute-start.79 = (f32[13,768]{1,0:T(8,128)}, f32[13,768]{1,0:T(8,128)}, u32[]{:S(2)}, u32[]{:S(2)}) collective-permute-start(f32[13,768]{1,0:T(8,128)} %add.576), channel_id=1, source_target_pairs={{0,2},{1,3},{2,0},{3,1},{4,6},{5,7},{6,4},{7,5},{8,10},{9,11},{10,... | collective-permute-start | bytes 119816 | tf_op jit(solution)/shard_map/ppermute | solution.py:341
  340.0 10.2 %collective-permute-start.80 = (f32[13,768]{1,0:T(8,128)}, f32[13,768]{1,0:T(8,128)}, u32[]{:S(2)}, u32[]{:S(2)}) collective-permute-start(f32[13,768]{1,0:T(8,128)} %add.576), channel_id=1, source_target_pairs={{0,3},{1,0},{2,1},{3,2},{4,7},{5,4},{6,5},{7,6},{8,11},{9,8},{10,9... | collective-permute-start | bytes 119816 | tf_op jit(solution)/shard_map/ppermute | solution.py:341
  350.2 32.7 %collective-permute-start.31 = (bf16[3,768,384]{2,1,0:T(8,128)(2,1)}, bf16[3,768,384]{2,1,0:T(8,128)(2,1)S(1)}, u32[]{:S(2)}, u32[]{:S(2)}) collective-permute-start(bf16[3,768,384]{2,1,0:T(8,128)(2,1)} %constant_dynamic-slice_fusion.12), channel_id=1, source_target_pairs={{0,4},{4,0},{8,12},{12,8},{16,20},{20,16},{24,28},{28,24},{1,5},{5... | collective-permute-start | bytes 5308424 | tf_op jit(solution)/shard_map/ppermute | solution.py:200
  374.8 36.6 %collective-permute-start.57 = (bf16[768,1536]{1,0:T(8,128)(2,1)S(1)}, bf16[768,1536]{1,0:T(8,128)(2,1)S(1)}, u32[]{:S(2)}, u32[]{:S(2)}) collective-permute-start(bf16[768,1536]{1,0:T(8,128)(2,1)S(1)} %copy-done.39), channel_id=1, source_target_pairs={{0,4},{4,0},{8,12},{12,8},{16,20},{20,16},{24,28},{28,24},{1,5},{5... | collective-permute-start | bytes 7077896 | tf_op jit(solution)/shard_map/ppermute | solution.py:200
  392.0 18.0 %collective-permute-start.34 = (bf16[3,4,2,48,256]{4,3,2,1,0:T(8,128)(2,1)S(1)}, bf16[3,4,2,48,256]{4,3,2,1,0:T(8,128)(2,1)S(1)}, u32[]{:S(2)}, u32[]{:S(2)}) collective-permute-start(bf16[3,4,2,48,256]{4,3,2,1,0:T(8,128)(2,1)S(1)} %dynamic-slice_bitcast_fusion.3), channel_id=1, source_target_pairs={{0,16},{4,20},{8,24},{12,28},{16,0},{20,4},{24,8},{28,12},{1,17},{... | collective-permute-start | bytes 1769480 | tf_op jit(solution)/shard_map/ppermute | solution.py:200
  401.8 49.5 %collective-permute-start.67 = (bf16[4,2,96,768]{3,2,1,0:T(8,128)(2,1)S(1)}, bf16[4,2,96,768]{3,2,1,0:T(8,128)(2,1)S(1)}, u32[]{:S(2)}, u32[]{:S(2)}) collective-permute-start(bf16[4,2,96,768]{3,2,1,0:T(8,128)(2,1)S(1)} %dynamic-slice_bitcast_fusion), channel_id=1, source_target_pairs={{0,16},{4,20},{8,24},{12,28},{16,0},{20,4},{24,8},{28,12},{1,17},{... | collective-permute-start | bytes 3538952 | tf_op jit(solution)/shard_map/ppermute | solution.py:200
  410.2 8.0 %collective-permute-start.35 = (bf16[3,4,48,256]{3,2,1,0:T(8,128)(2,1)S(1)}, bf16[3,4,48,256]{3,2,1,0:T(8,128)(2,1)S(1)}, u32[]{:S(2)}, u32[]{:S(2)}) collective-permute-start(bf16[3,4,48,256]{3,2,1,0:T(8,128)(2,1)S(1)} %dynamic-slice_bitcast_fusion.5), channel_id=1, source_target_pairs={{0,8},{4,12},{8,0},{12,4},{16,24},{20,28},{24,16},{28,20},{1,9},{5... | collective-permute-start | bytes 884744 | tf_op jit(solution)/shard_map/ppermute | solution.py:200
  418.4 8.8 %collective-permute-start.36 = (bf16[3,48,384]{2,1,0:T(8,128)(2,1)S(1)}, bf16[3,48,384]{2,1,0:T(8,128)(2,1)S(1)}, u32[]{:S(2)}, u32[]{:S(2)}) collective-permute-start(bf16[3,48,384]{2,1,0:T(8,128)(2,1)S(1)} %get-tuple-element.145), channel_id=1, source_target_pairs={{0,1},{1,2},{2,3},{3,0},{4,5},{5,6},{6,7},{7,4},{8,9},{9,10},{10,1... | collective-permute-start | bytes 331784 | tf_op jit(solution)/shard_map/ppermute | solution.py:190
  421.5 8.1 %collective-permute-start.37 = (bf16[3,48,384]{2,1,0:T(8,128)(2,1)S(1)}, bf16[3,48,384]{2,1,0:T(8,128)(2,1)S(1)}, u32[]{:S(2)}, u32[]{:S(2)}) collective-permute-start(bf16[3,48,384]{2,1,0:T(8,128)(2,1)S(1)} %get-tuple-element.146), channel_id=1, source_target_pairs={{0,2},{1,3},{2,0},{3,1},{4,6},{5,7},{6,4},{7,5},{8,10},{9,11},{10,... | collective-permute-start | bytes 331784 | tf_op jit(solution)/shard_map/ppermute | solution.py:190
  425.0 27.5 %collective-permute-start.58 = (bf16[768,768]{1,0:T(8,128)(2,1)S(1)}, bf16[768,768]{1,0:T(8,128)(2,1)S(1)}, u32[]{:S(2)}, u32[]{:S(2)}) collective-permute-start(bf16[768,768]{1,0:T(8,128)(2,1)S(1)} %pad_maximum_fusion.6), channel_id=1, source_target_pairs={{0,8},{4,12},{8,0},{12,4},{16,24},{20,28},{24,16},{28,20},{1,9},{5... | collective-permute-start | bytes 3538952 | tf_op jit(solution)/shard_map/ppermute | solution.py:200
  430.8 13.9 %collective-permute-start.39 = (bf16[3,48,128]{2,1,0:T(8,128)(2,1)S(1)}, bf16[3,48,128]{2,1,0:T(8,128)(2,1)S(1)}, u32[]{:S(2)}, u32[]{:S(2)}) collective-permute-start(bf16[3,48,128]{2,1,0:T(8,128)(2,1)S(1)} %get-tuple-element.169), channel_id=1, source_target_pairs={{0,8},{4,12},{8,0},{12,4},{16,24},{20,28},{24,16},{28,20},{1,9},{5... | collective-permute-start | bytes 110600 | tf_op jit(solution)/shard_map/ppermute | solution.py:200
  431.2 14.7 %collective-permute-start.41 = (bf16[3,48,256]{2,1,0:T(8,128)(2,1)S(1)}, bf16[3,48,256]{2,1,0:T(8,128)(2,1)S(1)}, u32[]{:S(2)}, u32[]{:S(2)}) collective-permute-start(bf16[3,48,256]{2,1,0:T(8,128)(2,1)S(1)} %get-tuple-element.172), channel_id=1, source_target_pairs={{0,16},{4,20},{8,24},{12,28},{16,0},{20,4},{24,8},{28,12},{1,17},{... | collective-permute-start | bytes 221192 | tf_op jit(solution)/shard_map/ppermute | solution.py:200
  451.6 15.8 %collective-permute-start.68 = (bf16[4,96,768]{2,1,0:T(8,128)(2,1)S(1)}, bf16[4,96,768]{2,1,0:T(8,128)(2,1)S(1)}, u32[]{:S(2)}, u32[]{:S(2)}) collective-permute-start(bf16[4,96,768]{2,1,0:T(8,128)(2,1)S(1)} %dynamic-slice_bitcast_fusion.1), channel_id=1, source_target_pairs={{0,8},{4,12},{8,0},{12,4},{16,24},{20,28},{24,16},{28,20},{1,9},{5... | collective-permute-start | bytes 1769480 | tf_op jit(solution)/shard_map/ppermute | solution.py:200
  453.0 18.8 %collective-permute-start.59 = (bf16[768,384]{1,0:T(8,128)(2,1)S(1)}, bf16[768,384]{1,0:T(8,128)(2,1)S(1)}, u32[]{:S(2)}, u32[]{:S(2)}) collective-permute-start(bf16[768,384]{1,0:T(8,128)(2,1)S(1)} %constant_dynamic-slice_fusion.3), channel_id=1, source_target_pairs={{0,16},{4,20},{8,24},{12,28},{16,0},{20,4},{24,8},{28,12},{1,17},{... | collective-permute-start | bytes 1769480 | tf_op jit(solution)/shard_map/ppermute | solution.py:200
  467.6 8.6 %collective-permute-start.69 = (bf16[96,768]{1,0:T(8,128)(2,1)S(1)}, bf16[96,768]{1,0:T(8,128)(2,1)S(1)}, u32[]{:S(2)}, u32[]{:S(2)}) collective-permute-start(bf16[96,768]{1,0:T(8,128)(2,1)S(1)} %get-tuple-element.123), channel_id=1, source_target_pairs={{0,1},{1,2},{2,3},{3,0},{4,5},{5,6},{6,7},{7,4},{8,9},{9,10},{10,1... | collective-permute-start | bytes 442376 | tf_op jit(solution)/shard_map/ppermute | solution.py:190
  468.6 17.8 %collective-permute-start.70 = (bf16[96,768]{1,0:T(8,128)(2,1)S(1)}, bf16[96,768]{1,0:T(8,128)(2,1)S(1)}, u32[]{:S(2)}, u32[]{:S(2)}) collective-permute-start(bf16[96,768]{1,0:T(8,128)(2,1)S(1)} %get-tuple-element.125), channel_id=1, source_target_pairs={{0,2},{1,3},{2,0},{3,1},{4,6},{5,7},{6,4},{7,5},{8,10},{9,11},{10,... | collective-permute-start | bytes 442376 | tf_op jit(solution)/shard_map/ppermute | solution.py:190
  471.4 15.1 %collective-permute-start.71 = (bf16[96,768]{1,0:T(8,128)(2,1)S(1)}, bf16[96,768]{1,0:T(8,128)(2,1)S(1)}, u32[]{:S(2)}, u32[]{:S(2)}) collective-permute-start(bf16[96,768]{1,0:T(8,128)(2,1)S(1)} %get-tuple-element.124), channel_id=1, source_target_pairs={{0,3},{1,0},{2,1},{3,2},{4,7},{5,4},{6,5},{7,6},{8,11},{9,8},{10,9... | collective-permute-start | bytes 442376 | tf_op jit(solution)/shard_map/ppermute | solution.py:190
  472.0 15.4 %collective-permute-start.60 = (bf16[192,384]{1,0:T(8,128)(2,1)S(1)}, bf16[192,384]{1,0:T(8,128)(2,1)S(1)}, u32[]{:S(2)}, u32[]{:S(2)}) collective-permute-start(bf16[192,384]{1,0:T(8,128)(2,1)S(1)} %get-tuple-element.140), channel_id=1, source_target_pairs={{0,1},{1,2},{2,3},{3,0},{4,5},{5,6},{6,7},{7,4},{8,9},{9,10},{10,1... | collective-permute-start | bytes 442376 | tf_op jit(solution)/shard_map/ppermute | solution.py:190
  473.7 20.3 %collective-permute-start.61 = (bf16[192,384]{1,0:T(8,128)(2,1)S(1)}, bf16[192,384]{1,0:T(8,128)(2,1)S(1)}, u32[]{:S(2)}, u32[]{:S(2)}) collective-permute-start(bf16[192,384]{1,0:T(8,128)(2,1)S(1)} %get-tuple-element.142), channel_id=1, source_target_pairs={{0,2},{1,3},{2,0},{3,1},{4,6},{5,7},{6,4},{7,5},{8,10},{9,11},{10,... | collective-permute-start | bytes 442376 | tf_op jit(solution)/shard_map/ppermute | solution.py:190
  476.2 17.7 %collective-permute-start.62 = (bf16[192,384]{1,0:T(8,128)(2,1)S(1)}, bf16[192,384]{1,0:T(8,128)(2,1)S(1)}, u32[]{:S(2)}, u32[]{:S(2)}) collective-permute-start(bf16[192,384]{1,0:T(8,128)(2,1)S(1)} %get-tuple-element.141), channel_id=1, source_target_pairs={{0,3},{1,0},{2,1},{3,2},{4,7},{5,4},{6,5},{7,6},{8,11},{9,8},{10,9... | collective-permute-start | bytes 442376 | tf_op jit(solution)/shard_map/ppermute | solution.py:190
  486.5 9.7 %collective-permute-start.72 = (bf16[96,768]{1,0:T(8,128)(2,1)S(1)}, bf16[96,768]{1,0:T(8,128)(2,1)S(1)}, u32[]{:S(2)}, u32[]{:S(2)}) collective-permute-start(bf16[96,768]{1,0:T(8,128)(2,1)S(1)} %fusion.40), channel_id=1, source_target_pairs={{0,8},{4,12},{8,0},{12,4},{16,24},{20,28},{24,16},{28,20},{1,9},{5... | collective-permute-start | bytes 442376 | tf_op jit(solution)/shard_map/ppermute | solution.py:200
  496.2 9.9 %collective-permute-start.73 = (bf16[2,96,768]{2,1,0:T(8,128)(2,1)S(1)}, bf16[2,96,768]{2,1,0:T(8,128)(2,1)S(1)}, u32[]{:S(2)}, u32[]{:S(2)}) collective-permute-start(bf16[2,96,768]{2,1,0:T(8,128)(2,1)S(1)} %maximum_select_fusion.22), channel_id=1, source_target_pairs={{0,16},{4,20},{8,24},{12,28},{16,0},{20,4},{24,8},{28,12},{1,17},{... | collective-permute-start | bytes 884744 | tf_op jit(solution)/shard_map/ppermute | solution.py:200
  499.7 11.5 %collective-permute-start.64 = (bf16[2,192,384]{2,1,0:T(8,128)(2,1)S(1)}, bf16[2,192,384]{2,1,0:T(8,128)(2,1)S(1)}, u32[]{:S(2)}, u32[]{:S(2)}) collective-permute-start(bf16[2,192,384]{2,1,0:T(8,128)(2,1)S(1)} %maximum_select_fusion.20), channel_id=1, source_target_pairs={{0,16},{4,20},{8,24},{12,28},{16,0},{20,4},{24,8},{28,12},{1,17},{... | collective-permute-start | bytes 884744 | tf_op jit(solution)/shard_map/ppermute | solution.py:200
  (79 other events, 974.3 us)
